TPU v7x, 32 devices: a whole 2x2x4 slice. The times are simulated.
32 devices in a mesh: dp: 4 (over z), ctx: 8 (over y, x, core).
Axes of the slice: x: 2, y: 2, z: 4, core: 2. Of those that a mesh axis runs over, the one named last changes fastest.
Arguments:
- features: bfloat16 [4, 1024, 4096], P('dp', 'ctx'), may hold values from -6 to 6
- short_weights: float32 [3, 3, 4096], replicated, may hold values from -3.5 to 3.5
- filters: bfloat16 [512, 256], replicated, may hold values from -0.25 to 0.25
- reach_panels: int32 [256], replicated, may hold values from 1 to 4, as said below
- cotangent: bfloat16 [4, 1024, 4096], P('dp', 'ctx'), may hold values from -6 to 6
Outputs:
- layer_out: bfloat16 [4, 1024, 4096], P('dp', 'ctx')
- input_grad: bfloat16 [4, 1024, 4096], P('dp', 'ctx')
- filter_grad: float32 [512, 256], replicated
- short_grad: float32 [3, 3, 4096], replicated
Inputs may be any that keep to these rules, and one draw needn't show every extreme that they name: `reach_panels`: each group's reach counts panels of 128 positions; some group reaches 4.
All inputs are finite; a program needn't handle non-finite values.
Results may differ from a plain program's by a relative error of at most 0.0051.
Values may be sent and summed in bfloat16 or wider, within the bound.
A program may use at most 128 MiB of HBM per device.

v0:
```python
import math

import jax
import jax.numpy as jnp
from jax import lax
from jax.sharding import PartitionSpec as P

PANEL = 128


def short_conv(extended, tap_weights):
    length = extended.shape[1] - 2
    return (
        tap_weights[0] * extended[:, 2:, :]
        + tap_weights[1] * extended[:, 1 : length + 1, :]
        + tap_weights[2] * extended[:, :length, :]
    )


def toeplitz_block(masked_t, offset, panel_rows):
    filter_len = masked_t.shape[1]
    lag_index = (
        offset * panel_rows
        + lax.broadcasted_iota(jnp.int32, (panel_rows, panel_rows), 0)
        - lax.broadcasted_iota(jnp.int32, (panel_rows, panel_rows), 1)
    )
    inside = (lag_index >= 0) & (lag_index < filter_len)
    picked = jnp.take(masked_t, jnp.clip(lag_index, 0, filter_len - 1), axis=1)
    return jnp.where(inside[None, :, :], picked, jnp.zeros((), masked_t.dtype))


def lag_sums(blocks):
    groups, panel_rows = (blocks.shape[0], blocks.shape[1])
    flipped = blocks[:, :, ::-1]
    padded = jnp.pad(flipped, ((0, 0), (0, 0), (0, panel_rows)))
    flattened = padded.reshape(groups, 2 * panel_rows * panel_rows)[
        :, : panel_rows * (2 * panel_rows - 1)
    ]
    return jnp.sum(flattened.reshape(groups, panel_rows, 2 * panel_rows - 1), axis=1)


def long_conv(ext_mixed, ext_grads, grad_own, filter_rows, reach_max):
    seq_rows, own_rows, width = grad_own.shape
    units = filter_rows.shape[0]
    unit_width = width // units
    filter_len = filter_rows.shape[1]
    own_panels = own_rows // PANEL
    ext_panels = own_panels + reach_max - 1

    def to_units(values, panels):
        split = values.reshape(seq_rows, panels, PANEL, units, unit_width).transpose(3, 0, 4, 1, 2)
        return split.reshape(units, seq_rows * unit_width, panels, PANEL)

    def from_units(values):
        split = values.reshape(units, seq_rows, unit_width, own_panels, PANEL).transpose(
            1, 3, 4, 0, 2
        )
        return split.reshape(seq_rows, own_rows, width)

    own_split = to_units(grad_own, own_panels)
    mixed_split = to_units(ext_mixed, ext_panels)
    grads_split = to_units(ext_grads, ext_panels)
    total = jnp.zeros(own_split.shape, jnp.float32)
    back = jnp.zeros(own_split.shape, jnp.float32)
    accum = jnp.zeros((units, filter_len + 2 * PANEL), jnp.float32)
    for offset in range(reach_max):
        block = toeplitz_block(filter_rows, offset, PANEL)
        earlier = mixed_split[:, :, reach_max - 1 - offset : reach_max - 1 - offset + own_panels]
        later = grads_split[:, :, offset : offset + own_panels]
        total = total + jnp.einsum(
            "uts,umns->umnt", block, earlier, preferred_element_type=jnp.float32
        )
        back = back + jnp.einsum("uts,umnt->umns", block, later, preferred_element_type=jnp.float32)
        products = jnp.einsum(
            "umnt,umns->uts", own_split, earlier, preferred_element_type=jnp.float32
        )
        accum = accum.at[:, offset * PANEL + 1 : offset * PANEL + 2 * PANEL].add(lag_sums(products))
    return (from_units(total), from_units(back), accum[:, PANEL : PANEL + filter_len].T)


def input_taps(weights, grad_ext, rows):
    grad_in = jnp.zeros(grad_ext.shape[1:2] + (rows,) + grad_ext.shape[3:], jnp.float32)
    for stream in range(3):
        for tap in range(3):
            grad_in = grad_in + weights[stream, tap] * grad_ext[stream, :, tap : tap + rows, :]
    return grad_in


def short_terms(stacked, extended, rows):
    return jnp.stack(
        [
            jnp.stack(
                [
                    jnp.sum(stacked[stream] * extended[:, 2 - tap : 2 - tap + rows, :], axis=(0, 1))
                    for tap in range(3)
                ]
            )
            for stream in range(3)
        ]
    )


def shards(features, short_weights, filters, reach_panels, cotangent):
    filter_len, groups = filters.shape
    channels = features.shape[2]
    reach_max = filter_len // PANEL
    margin = (reach_max - 1) * PANEL
    lag_pos = lax.broadcasted_iota(jnp.int32, (filter_len, groups), 0)
    keep = lag_pos < reach_panels[None, :] * PANEL
    masked = jnp.where(keep, filters, jnp.zeros((), filters.dtype))
    masked_t = masked.T
    inputs_local, cot_local = (
        lax.all_to_all(features, "ctx", split_axis=2, concat_axis=1, tiled=True),
        lax.all_to_all(cotangent, "ctx", split_axis=2, concat_axis=1, tiled=True),
    )
    seq_rows, length, local_width = inputs_local.shape
    first_channel = lax.axis_index("ctx") * local_width
    weights = lax.dynamic_slice_in_dim(short_weights, first_channel, local_width, 2)
    unit_width = math.gcd(local_width, 16)
    group_ids = (
        first_channel + jnp.arange(local_width // unit_width, dtype=jnp.int32) * unit_width
    ) // 16
    filter_rows = jnp.take(masked_t, group_ids, axis=0)
    extended = jnp.pad(inputs_local.astype(jnp.float32), ((0, 0), (2, 0), (0, 0)))
    queries = short_conv(extended, weights[0])
    key_feat = short_conv(extended, weights[1])
    value_feat = short_conv(extended, weights[2])
    mixed = (key_feat * value_feat).astype(jnp.bfloat16)
    cot_float = cot_local.astype(jnp.float32)
    grad_conv = (cot_float * queries).astype(jnp.bfloat16)
    ext_mixed = jnp.pad(mixed, ((0, 0), (margin, 0), (0, 0)))
    ext_grads = jnp.pad(grad_conv, ((0, 0), (0, margin), (0, 0)))
    conv_out, grad_mixed, unit_grad = long_conv(
        ext_mixed, ext_grads, grad_conv, filter_rows, reach_max
    )
    layer_local = (queries * conv_out).astype(jnp.bfloat16)
    stacked = jnp.stack([cot_float * conv_out, grad_mixed * value_feat, grad_mixed * key_feat])
    grad_ext = jnp.pad(stacked, ((0, 0), (0, 0), (0, 2), (0, 0)))
    grad_in = input_taps(weights, grad_ext, length).astype(jnp.bfloat16)
    short_local = short_terms(stacked, extended, length)
    layer_out, input_grad = (
        lax.all_to_all(layer_local, "ctx", split_axis=1, concat_axis=2, tiled=True),
        lax.all_to_all(grad_in, "ctx", split_axis=1, concat_axis=2, tiled=True),
    )
    chooser = (
        group_ids[:, None] == lax.broadcasted_iota(jnp.int32, (group_ids.shape[0], groups), 1)
    ).astype(jnp.float32)
    filter_part = jnp.dot(
        unit_grad, chooser, precision=lax.Precision.HIGHEST, preferred_element_type=jnp.float32
    )
    zero_index = jnp.zeros((), jnp.int32)
    short_part = lax.dynamic_update_slice(
        jnp.zeros((3, 3, channels), jnp.float32),
        short_local,
        (zero_index, zero_index, first_channel),
    )
    filter_sum, short_grad = lax.psum((filter_part, short_part), ("dp", "ctx"))
    filter_grad = jnp.where(keep, filter_sum, jnp.zeros((), jnp.float32))
    return (layer_out, input_grad, filter_grad, short_grad)


def solution(mesh):
    return jax.shard_map(
        shards,
        mesh=mesh,
        in_specs=(P("dp", "ctx", None), P(), P(), P(), P("dp", "ctx", None)),
        out_specs=(P("dp", "ctx", None), P("dp", "ctx", None), P(), P()),
        check_vma=False,
    )
```

profile of v0, /device:TPU:0, one launch (start us, length us, event | category | flops | bytes accessed | tf_op | source)
XLA Modules:
  0.0 821.4 jit_solution(15978120117579027378)
XLA Ops:
  7.2 5.0 copy.97
  12.7 22.4 %reduce.33 = bf16[4096,128]{1,0:T(8,128)(2,1)S(1)} reduce(bf16[4096,1,128]{2,1,0:T(2,128)(2,1)S(1)} %bitcast.314, bf16[]{:T(256)} %broadcast.689), dimensions={1}, to_apply=%bitcast.267.reduce_sub_computation | reduce | bytes 2097154
  36.2 5.6 all-to-all-start
  41.9 2.8 copy.112
  44.8 22.4 %reduce.34 = bf16[4096,128]{1,0:T(8,128)(2,1)S(1)} reduce(bf16[4096,1,128]{2,1,0:T(2,128)(2,1)S(1)} %bitcast.318, bf16[]{:T(256)} %broadcast.689), dimensions={1}, to_apply=%bitcast.271.reduce_sub_computation | reduce | bytes 2097154
  69.5 57.8 %gather_fusion.4 = bf16[16384,32]{1,0:T(8,128)(2,1)} fusion(bf16[32,512]{0,1:T(8,128)(2,1)S(1)} %copy.102, s32[16384]{0:T(1024)S(1)} %bitcast_clamp_fusion), kind=kCustom, calls=%fused_computation.3.clone | custom fusion | bytes 2162688 | tf_op jit(solution)/shard_map/jit(_take)/gather | solution.py:28
  127.4 4.0 copy.109
  131.5 57.8 %gather_fusion.3 = bf16[16384,32]{1,0:T(8,128)(2,1)} fusion(bf16[32,512]{0,1:T(8,128)(2,1)S(1)} %copy.102, s32[16384]{0:T(1024)S(1)} %bitcast_clamp_fusion.1), kind=kCustom, calls=%fused_computation.2.clone | custom fusion | bytes 2162688 | tf_op jit(solution)/shard_map/jit(_take)/gather | solution.py:28
  189.3 4.9 copy.107
  194.2 57.8 %gather_fusion.1 = bf16[16384,32]{1,0:T(8,128)(2,1)} fusion(bf16[32,512]{0,1:T(8,128)(2,1)S(1)} %copy.102, s32[16384]{0:T(1024)S(1)} %bitcast_clamp_fusion.3), kind=kCustom, calls=%fused_computation.clone | custom fusion | bytes 2162688 | tf_op jit(solution)/shard_map/jit(_take)/gather | solution.py:28
  252.1 4.9 copy.103
  257.1 57.9 %gather_fusion.2 = bf16[16384,32]{1,0:T(8,128)(2,1)} fusion(bf16[32,512]{0,1:T(8,128)(2,1)S(1)} %copy.102, s32[16384]{0:T(1024)S(1)} %bitcast_clamp_fusion.2), kind=kCustom, calls=%fused_computation.1.clone | custom fusion | bytes 2162688 | tf_op jit(solution)/shard_map/jit(_take)/gather | solution.py:28
  315.0 4.9 copy.105
  323.8 4.5 all-to-all-start.2
  328.4 4.3 reshape.945
  337.6 6.1 all-to-all-done.2
  343.7 4.3 reshape.949
  352.8 3.6 copy.99
  356.4 4.2 copy.114
  360.6 13.7 %multiply_convert_fusion.1 = (bf16[1,1024,512]{2,0,1:T(2,128)(2,1)}, f32[1,1024,512]{2,0,1:T(1,128)}, f32[1,1024,512]{2,0,1:T(1,128)}, bf16[1,1024,512]{2,0,1:T(2,128)(2,1)}, f32[1,1024,512]{2,0,1:T(1,128)}) fusion(f32[512]{0:T(512)S(1)} %bitcast.356, f32[1,1024,512]{2,0,1:T(1,128)S(1)} %bitcast.288, f32[512]{0:T(512)S(1)} %bitcast.342, ...), kind=kLoop, calls=%fused_computation.44 | loop fusion | flops 9961472 | bytes 14698496 | tf_op jit(solution)/shard_map/convert_element_type | solution.py:128
  374.2 5.8 copy.135
  382.5 3.9 reshape.843
  386.4 5.8 copy.136
  394.7 3.9 reshape.848
  398.6 2.9 fusion.30
  410.6 2.9 multiply_reduce_fusion.8
  416.2 3.1 reshape.847
  428.9 6.0 copy.110
  434.9 5.4 add_bitcast_fusion
  443.1 6.0 copy.119
  449.1 19.5 %multiply_reduce_fusion.7 = (f32[512]{0:T(512)S(1)}, f32[512]{0:T(512)S(1)}, f32[512]{0:T(512)S(1)}, f32[512]{0:T(512)S(1)}, f32[512]{0:T(512)S(1)}, /*index=5*/...) fusion(f32[1,1024,512]{2,0,1:T(1,128)} %copy.110, ...), kind=kLoop, calls=%fused_computation.39 | loop fusion | flops 11005952 | bytes 22036480 | tf_op jit(solution)/shard_map/reduce_sum | solution.py:94
  468.6 8.0 reduce.35
  478.3 3.7 all-to-all-start.1
  482.0 6.2 copy.117
  491.1 9.3 %select_maximum_fusion = f32[3,1,1026,512]{3,0,2,1:T(4,128)S(1)} fusion(f32[1,1,1024,512]{3,0,2,1:T(1,128)S(1)} %bitcast.296, f32[1,1,1024,512]{3,0,2,1:T(1,128)S(1)} %bitcast.295, f32[1,1,1024,512]{3,0,2,1:T(1,128)S(1)} %bitcast.317), kind=kLoop, calls=%fused_computation.5 | loop fusion | flops 9455616 | bytes 12595200 | tf_op jit(solution)/shard_map/stack | solution.py:137
  500.3 15.9 %fusion.15 = bf16[1,1024,512]{2,0,1:T(2,128)(2,1)} fusion(f32[3,1,1026,512]{3,0,2,1:T(4,128)S(1)} %select_maximum_fusion, f32[1,1024,512]{2,0,1:T(1,128)S(1)} %copy-done.5, f32[1,1024,512]{2,0,1:T(1,128)S(1)} %copy-done.4, f32[512]{0:T(512)S(1)} %bitcast.357, f32[512]{0:T(512)S(1)} %bitcast.343, f32[512]{0:T(512)S(1)} %bitcast.345, f32[512]{0:T(512)S(1)} %bitcast.347, ...), kind=kLoop, calls=%fused_computation.48 | loop fusion | flops 9961472 | bytes 22038528 | tf_op jit(solution)/shard_map/convert_element_type | solution.py:139
  516.2 8.0 reduce.36
  525.8 15.1 %rev.12 = f32[32,128,128]{2,1,0:T(8,128)S(1)} reverse(f32[32,128,128]{2,1,0:T(8,128)} %convolution_bitcast_fusion.3), dimensions={2} | reverse | bytes 4194304 | tf_op jit(solution)/shard_map/rev | solution.py:34
  546.1 9.4 %reshape.855 = f32[32,128,255]{2,1,0:T(8,128)} reshape(f32[32,32640]{1,0:T(8,128)} %slice.272) | data formatting | bytes 8355840 | tf_op jit(solution)/shard_map/reshape | solution.py:39
  558.9 14.9 %rev.13 = f32[32,128,128]{2,1,0:T(8,128)S(1)} reverse(f32[32,128,128]{2,1,0:T(8,128)} %convolution_bitcast_fusion.2), dimensions={2} | reverse | bytes 4194304 | tf_op jit(solution)/shard_map/rev | solution.py:34
  579.0 9.4 %reshape.857 = f32[32,128,255]{2,1,0:T(8,128)} reshape(f32[32,32640]{1,0:T(8,128)} %slice.273) | data formatting | bytes 8355840 | tf_op jit(solution)/shard_map/reshape | solution.py:39
  591.0 15.3 %rev.14 = f32[32,128,128]{2,1,0:T(8,128)S(1)} reverse(f32[32,128,128]{2,1,0:T(8,128)} %convolution_bitcast_fusion.1), dimensions={2} | reverse | bytes 4194304 | tf_op jit(solution)/shard_map/rev | solution.py:34
  611.5 9.4 %reshape.859 = f32[32,128,255]{2,1,0:T(8,128)} reshape(f32[32,32640]{1,0:T(8,128)} %slice.275) | data formatting | bytes 8355840 | tf_op jit(solution)/shard_map/reshape | solution.py:39
  623.6 14.9 %rev.15 = f32[32,128,128]{2,1,0:T(8,128)S(1)} reverse(f32[32,128,128]{2,1,0:T(8,128)} %convolution_bitcast_fusion), dimensions={2} | reverse | bytes 4194304 | tf_op jit(solution)/shard_map/rev | solution.py:34
  643.7 9.4 %reshape.861 = f32[32,128,255]{2,1,0:T(8,128)} reshape(f32[32,32640]{1,0:T(8,128)} %slice.277) | data formatting | bytes 8355840 | tf_op jit(solution)/shard_map/reshape | solution.py:39
  659.8 4.3 all-to-all-start.3
  665.5 136.4 %all-reduce.12.cloned.1.call-done = (f32[512,256]{1,0:T(8,128)}, f32[3,3,4096]{2,1,0:T(4,128)}) async-done(((f32[512,256]{1,0:T(8,128)}, f32[3,3,4096]{2,1,0:T(4,128)}), (f32[512,256]{1,0:T(8,128)}, f32[3,3,4096]{2,1,0:T(4,128)})) %all-reduce.12.cloned.1.call-update) | async-done | bytes 671760 | tf_op jit(solution)/shard_map/psum | solution.py:157
  807.1 4.3 reshape.951
  (129 shorter events, 98.1 us)
Async XLA Ops:
  36.2 5.7 copy-start.10
  36.2 287.6 %all-to-all-start = ((bf16[8,2,32768]{2,1,0:T(2,128)(2,1)}), bf16[8,2,32768]{2,1,0:T(2,128)(2,1)}, u32[]{:S(2)}, u32[]{:S(2)}) async-start(bf16[8,2,32768]{2,1,0:T(2,128)(2,1)} %reshape.944), calls=%async_computation | async-start | bytes 2097152 | tf_op jit(solution)/shard_map/all_to_all | solution.py:113
  44.8 23.6 %copy-start.16 = (s32[256]{0:T(256)S(1)}, s32[256]{0:T(256)}, u32[]{:S(2)}) copy-start(s32[256]{0:T(256)} %param.18) | copy-start | bytes 3076
  44.8 23.6 %copy-start.14 = (bf16[512,256]{1,0:T(8,128)(2,1)S(1)}, bf16[512,256]{1,0:T(8,128)(2,1)}, u32[]{:S(2)}) copy-start(bf16[512,256]{1,0:T(8,128)(2,1)} %param.17) | copy-start | bytes 786436
  323.8 19.9 %all-to-all-start.2 = ((bf16[8,2,32768]{2,1,0:T(2,128)(2,1)}), bf16[8,2,32768]{2,1,0:T(2,128)(2,1)}, u32[]{:S(2)}, u32[]{:S(2)}) async-start(bf16[8,2,32768]{2,1,0:T(2,128)(2,1)} %reshape.948), calls=%async_computation.2 | async-start | bytes 2097152 | tf_op jit(solution)/shard_map/all_to_all | solution.py:114
  398.6 2.9 copy-start.6
  398.6 2.9 copy-start.12
  401.5 1.9 copy-start.7
  401.5 2.6 copy-start.9
  404.9 1.8 copy-start.11
  407.6 1.9 copy-start.1
  407.6 3.0 copy-start.2
  419.3 1.9 copy-start.8
  478.3 181.5 %all-to-all-start.1 = ((bf16[8,2,32768]{2,1,0:T(2,128)(2,1)}), bf16[8,2,32768]{2,1,0:T(2,128)(2,1)S(1)}, u32[]{:S(2)}, u32[]{:S(2)}) async-start(bf16[8,2,32768]{2,1,0:T(2,128)(2,1)} %reshape.946), calls=%async_computation.1 | async-start | bytes 2097152 | tf_op jit(solution)/shard_map/all_to_all | solution.py:142
  482.0 6.2 copy-start
  488.2 2.3 copy-start.4
  488.2 2.9 copy-start.5
  491.0 9.3 %copy-start.3 = (f32[1,1024,512]{2,0,1:T(1,128)S(1)}, f32[1,1024,512]{2,0,1:T(1,128)}, u32[]{:S(2)}) copy-start(f32[1,1024,512]{2,0,1:T(1,128)} %copy.110) | copy-start | bytes 6291460
  659.8 147.2 %all-to-all-start.3 = ((bf16[8,2,32768]{2,1,0:T(2,128)(2,1)}), bf16[8,2,32768]{2,1,0:T(2,128)(2,1)}, u32[]{:S(2)}, u32[]{:S(2)}) async-start(bf16[8,2,32768]{2,1,0:T(2,128)(2,1)} %reshape.950), calls=%async_computation.3 | async-start | bytes 2097152 | tf_op jit(solution)/shard_map/all_to_all | solution.py:143
  664.1 137.8 %all-reduce.12.cloned.1.call-start = ((), (), s32[]{:S(2)}) async-start(), calls=%async_computation.4 | async-start | bytes 1441792 | tf_op jit(solution)/shard_map/psum | solution.py:157
  664.2 1.2 copy-start.13
  811.7 2.0 copy-start.15
Sparse Core Ops, SparseCore 0:
  670.7 131.0 all-reduce.11
where the time goes:
time: 832 us; the launch traced here: 821 us
  local copies, waits for them, and re-layouts  474 us (57%)
  other arithmetic  144 us (17%)
  waiting for transfers between devices  143 us (17%)
  matrix products  27.2 us (3%)
  starting transfers between devices  18.1 us (2%)
  between operations  14.9 us (2%)
    gather x8, local copies, waits for them, and re-layouts, toeplitz_block(): picked = jnp.take(masked_t, jnp.clip(lag_index, 0, filter_len - 1), axis=1)  250 us
    psum x1, waiting for transfers between devices, shards(): filter_sum, short_grad = lax.psum((filter_part, short_part), ('dp', 'ctx'))  136 us
    unnamed x4, other arithmetic  60.9 us
    rev x4, local copies, waits for them, and re-layouts, lag_sums(): flipped = blocks[:, :, ::-1]  60.3 us
    unnamed x57, local copies, waits for them, and re-layouts  57.5 us
    reshape x4, local copies, waits for them, and re-layouts, lag_sums(): flattened.reshape(groups, panel_rows, 2 * panel_rows - 1)  37.7 us
    reshape x6, local copies, waits for them, and re-layouts, from_units(): return split.reshape(seq_rows, own_rows, width)  26.8 us
    reduce_sum x1, other arithmetic, short_terms(): jnp.sum(stacked[stream] * extended[:, 2 - tap:2 - tap + rows, :], axis=(0...  19.5 us
  transfers between devices with their start and end apart: 5, of which 2 were waited for; matrix products, arithmetic and copies ran while one was open for 58% of the time, Pallas kernels for 0%

commit v1 on v0

v1 whole, which is shorter than its diff:
```python
import functools

import jax
import jax.numpy as jnp
from jax import lax
from jax.experimental import pallas as pl
from jax.experimental.pallas import tpu as pltpu
from jax.sharding import PartitionSpec as P

PANEL = 128
UNIT = 16
TILE = 128
TAPS = 3


def rows_down(x, rows):
    return jnp.concatenate([jnp.zeros((rows, x.shape[1]), x.dtype), x[:-rows]], axis=0)


def rows_up(x, rows):
    return jnp.concatenate([x[rows:], jnp.zeros((rows, x.shape[1]), x.dtype)], axis=0)


def toeplitz(taps):
    width = taps.shape[1]
    x = jnp.broadcast_to(taps, (8, width))
    row = lax.broadcasted_iota(jnp.int32, (8, width), 0)
    for bit in (1, 2, 4):
        x = jnp.where((row & bit) != 0, pltpu.roll(x, bit, 1), x)
    rows = 8
    while rows < PANEL:
        x = jnp.concatenate([x, pltpu.roll(x, rows, 1)], axis=0)
        rows *= 2
    return x


def causal():
    shape = (PANEL, PANEL)
    return lax.broadcasted_iota(jnp.int32, shape, 1) >= lax.broadcasted_iota(jnp.int32, shape, 0)


def lag_sums(products):
    width = products.shape[1]
    first = jnp.where(causal(), products[:, :PANEL], 0.0)
    x = jnp.concatenate([first, products[:, PANEL:]], axis=1)
    rows = PANEL // 2
    while rows >= 8:
        x = x[:rows] + pltpu.roll(x[rows:], width - rows, 1)
        rows //= 2
    for step in (4, 2, 1):
        x = x + pltpu.roll(pltpu.roll(x, 8 - step, 0), width - step, 1)
    return x[0:1]


def tile_terms(reach, panels, ft, ct, wt, taps, mixed_ext, grads_ext, out_t, in_t, fg, sg_t):
    rows = panels * UNIT
    pad = (reach - 1) * UNIT
    mixed_ext[0:pad, :] = jnp.zeros((pad, PANEL), jnp.bfloat16)
    grads_ext[rows : rows + pad, :] = jnp.zeros((pad, PANEL), jnp.bfloat16)

    def group(g, carry):
        first = pl.multiple_of(g * UNIT, UNIT)
        lane = lax.broadcasted_iota(jnp.int32, (rows, PANEL), 1)
        chan = pl.ds(first, UNIT)
        feat = ft[:, chan, :].reshape(rows, PANEL)
        cot = ct[:, chan, :].reshape(rows, PANEL)
        w_all = wt[chan, :]

        def weigh(k, x):
            w = jnp.broadcast_to(w_all[:, k : k + 1], (UNIT, PANEL))
            return (x.reshape(panels, UNIT, PANEL) * w[None]).reshape(rows, PANEL)

        feats = [feat]
        for tap in range(1, TAPS):
            turned = pltpu.roll(feat, tap, 1)
            feats.append(jnp.where(lane < tap, rows_down(turned, UNIT), turned))
        streams = []
        for m in range(3):
            total = weigh(m * TAPS, feats[0])
            for tap in range(1, TAPS):
                total = total + weigh(m * TAPS + tap, feats[tap])
            streams.append(total)
        query, key, value = streams
        mixed = (key * value).astype(jnp.bfloat16)
        grad_conv = (cot * query).astype(jnp.bfloat16)
        mixed_ext[pad : pad + rows, :] = mixed
        grads_ext[0:rows, :] = grad_conv
        earlier = jnp.concatenate(
            [mixed_ext[pad - o * UNIT : pad - o * UNIT + rows, :] for o in range(reach)], axis=1
        )
        later = jnp.concatenate(
            [grads_ext[o * UNIT : o * UNIT + rows, :] for o in range(reach)], axis=1
        )
        spread = toeplitz(taps[pl.ds(g, 1), :])
        spread = jnp.concatenate(
            [jnp.where(causal(), spread[:, :PANEL], 0.0), spread[:, PANEL:]], axis=1
        ).astype(jnp.bfloat16)
        stacked = jnp.concatenate(
            [spread[:, o * PANEL : (o + 1) * PANEL] for o in range(reach)], axis=0
        )
        conv = jnp.dot(earlier, stacked, preferred_element_type=jnp.float32)
        back = lax.dot_general(
            later, spread, (((1,), (1,)), ((), ())), preferred_element_type=jnp.float32
        )
        products = lax.dot_general(
            mixed, later, (((0,), (0,)), ((), ())), preferred_element_type=jnp.float32
        )
        fg[pl.ds(g, 1), :] = lag_sums(products)
        out_t[:, chan, :] = (query * conv).reshape(panels, UNIT, PANEL)
        grads = (cot * conv, back * value, back * key)
        grad_in = None
        for tap in range(TAPS):
            part = weigh(tap, grads[0]) + weigh(TAPS + tap, grads[1]) + weigh(2 * TAPS + tap, grads[2])
            if tap:
                turned = pltpu.roll(part, PANEL - tap, 1)
                part = jnp.where(lane >= PANEL - tap, rows_up(turned, UNIT), turned)
            grad_in = part if grad_in is None else grad_in + part
        in_t[:, chan, :] = grad_in.reshape(panels, UNIT, PANEL)
        small_lane = lax.broadcasted_iota(jnp.int32, (UNIT, PANEL), 1)
        sums = jnp.zeros((UNIT, PANEL), jnp.float32)
        for m in range(3):
            for tap in range(TAPS):
                part = jnp.sum((grads[m] * feats[tap]).reshape(panels, UNIT, PANEL), axis=0)
                sums = jnp.where(small_lane == m * TAPS + tap, jnp.sum(part, axis=1, keepdims=True), sums)
        sg_t[chan, :] = sums
        return carry

    lax.fori_loop(0, TILE // UNIT, group, 0)


def local_kernel(reach, panels, f_ref, c_ref, wt, taps, out_ref, in_ref, fg, sg, ft, ct, out_t, in_t, sg_t, mixed_ext, grads_ext):
    def turn_in(n, carry):
        rows = pl.ds(pl.multiple_of(n * PANEL, PANEL), PANEL)
        ft[n] = f_ref[rows, :].astype(jnp.float32).T
        ct[n] = c_ref[rows, :].astype(jnp.float32).T
        return carry

    lax.fori_loop(0, panels, turn_in, 0)
    tile_terms(reach, panels, ft, ct, wt, taps, mixed_ext, grads_ext, out_t, in_t, fg, sg_t)
    sg[...] = sg_t[...].T[:UNIT]

    def turn_out(n, carry):
        rows = pl.ds(pl.multiple_of(n * PANEL, PANEL), PANEL)
        out_ref[rows, :] = out_t[n].T.astype(jnp.bfloat16)
        in_ref[rows, :] = in_t[n].T.astype(jnp.bfloat16)
        return carry

    lax.fori_loop(0, panels, turn_out, 0)


def shards(features, short_weights, filters, reach_panels, cotangent):
    filter_len, groups = filters.shape
    channels = features.shape[2]
    reach = filter_len // PANEL
    lag_pos = lax.broadcasted_iota(jnp.int32, (filter_len, groups), 0)
    keep = lag_pos < reach_panels[None, :] * PANEL
    masked = jnp.where(keep, filters, jnp.zeros((), filters.dtype))
    f_all = lax.all_to_all(features[0], "ctx", split_axis=1, concat_axis=0, tiled=True)
    c_all = lax.all_to_all(cotangent[0], "ctx", split_axis=1, concat_axis=0, tiled=True)
    length, width = f_all.shape
    panels = length // PANEL
    me = lax.axis_index("ctx")
    units = width // UNIT
    taps = lax.dynamic_slice_in_dim(masked, me * units, units, 1).T.astype(jnp.float32)
    wt = lax.dynamic_slice_in_dim(short_weights.reshape(9, channels), me * width, width, 1).T
    tile_units = TILE // UNIT
    big = lambda: pl.BlockSpec((length, TILE), lambda j: (0, j))
    out_local, in_local, fg, sg = pl.pallas_call(
        functools.partial(local_kernel, reach, panels),
        grid=(width // TILE,),
        in_specs=[
            big(),
            big(),
            pl.BlockSpec((TILE, 9), lambda j: (j, 0)),
            pl.BlockSpec((tile_units, filter_len), lambda j: (j, 0)),
        ],
        out_specs=[
            big(),
            big(),
            pl.BlockSpec((tile_units, filter_len), lambda j: (j, 0)),
            pl.BlockSpec((UNIT, TILE), lambda j: (0, j)),
        ],
        out_shape=[
            jax.ShapeDtypeStruct((length, width), jnp.bfloat16),
            jax.ShapeDtypeStruct((length, width), jnp.bfloat16),
            jax.ShapeDtypeStruct((units, filter_len), jnp.float32),
            jax.ShapeDtypeStruct((UNIT, width), jnp.float32),
        ],
        scratch_shapes=[pltpu.VMEM((panels, TILE, PANEL), jnp.float32)] * 4
        + [
            pltpu.VMEM((TILE, PANEL), jnp.float32),
            pltpu.VMEM(((panels + reach - 1) * UNIT, PANEL), jnp.bfloat16),
            pltpu.VMEM(((panels + reach - 1) * UNIT, PANEL), jnp.bfloat16),
        ],
        compiler_params=pltpu.CompilerParams(vmem_limit_bytes=40 * 2**20),
    )(f_all, c_all, wt, taps)
    layer_out = lax.all_to_all(out_local, "ctx", split_axis=0, concat_axis=1, tiled=True)[None]
    input_grad = lax.all_to_all(in_local, "ctx", split_axis=0, concat_axis=1, tiled=True)[None]
    flat = jnp.concatenate([fg.reshape(-1), sg[:9].reshape(-1)])
    flat = lax.psum(flat, "dp")
    every = lax.all_gather(flat, "ctx")
    cut = units * filter_len
    filter_sum = every[:, :cut].reshape(groups, filter_len).T
    filter_grad = jnp.where(keep, filter_sum, jnp.zeros((), jnp.float32))
    short_grad = every[:, cut:].reshape(-1, 9, width).transpose(1, 0, 2).reshape(3, 3, channels)
    return (layer_out, input_grad, filter_grad, short_grad)


def solution(mesh):
    return jax.shard_map(
        shards,
        mesh=mesh,
        in_specs=(P("dp", "ctx", None), P(), P(), P(), P("dp", "ctx", None)),
        out_specs=(P("dp", "ctx", None), P("dp", "ctx", None), P(), P()),
        check_vma=False,
    )
```

time: 832 us -> 186 us (0.22); the launches traced: 821 us -> 185 us
  local copies, waits for them, and re-layouts: 474 us -> 13.2 us
  other arithmetic: 144 us -> 0.94 us
  waiting for transfers between devices: 143 us -> 65.5 us
  Pallas kernels: 0 us -> 50.7 us
  blocking collectives: 0 us -> 28.2 us
  matrix products: 27.2 us -> 0 us
    gather x9 -> x0, local copies, waits for them, and re-layouts: 251 us -> none  [the longest x8 250 us: toeplitz_block(): picked = jnp.take(masked_t, jnp.clip(lag_index, 0, filter_len - 1), axis=1)]
    psum x1, waiting for transfers between devices: 136 us -> 38.8 us  [shards(): flat = lax.psum(flat, 'dp')]
    reshape x12 -> x4, local copies, waits for them, and re-layouts: 72.4 us -> 0.96 us  [the longest x1 0.79 us: shards(): every[:, cut:].reshape(-1, 9, width).transpose(1, 0, 2)]
    unnamed x4 -> x0, other arithmetic: 60.9 us -> none
    rev x4 -> x0, local copies, waits for them, and re-layouts: 60.3 us -> none  [lag_sums(): flipped = blocks[:, :, ::-1]]
    unnamed x57 -> x19, local copies, waits for them, and re-layouts: 57.5 us -> 5.01 us
    pallas_call x0 -> x1, Pallas kernels: none -> 50.7 us  [shards(): pl.pallas_call(functools.partial(local_kernel, reach, panels), grid=(widt...]
    convert_element_type x4 -> x1, other arithmetic: 34 us -> 0.01 us  [shards(): lax.dynamic_slice_in_dim(masked, me * units, units, 1).T.astype(jnp.float32)]
  transfers between devices with their start and end apart: 5 -> 4, of which waited for: 2 -> 3; matrix products, arithmetic and copies ran while one was open for 58% -> 4% of each run, Pallas kernels for 0% -> 0%
where the time goes in v1:
time: 186 us; the launch traced here: 185 us
  waiting for transfers between devices  65.5 us (35%)
  Pallas kernels  50.7 us (27%)
  blocking collectives  28.2 us (15%)
  between operations  14.2 us (8%)
  local copies, waits for them, and re-layouts  13.2 us (7%)
  starting transfers between devices  12.5 us (7%)
    pallas_call x1, Pallas kernels, shards(): pl.pallas_call(functools.partial(local_kernel, reach, panels), grid=(widt...  50.7 us
    psum x1, waiting for transfers between devices, shards(): flat = lax.psum(flat, 'dp')  38.8 us
    all_to_all x1, blocking collectives, shards(): lax.all_to_all(in_local, 'ctx', split_axis=0, concat_axis=1, tiled=True)  17.8 us
    all_to_all x1, waiting for transfers between devices, shards(): lax.all_to_all(features[0], 'ctx', split_axis=1, concat_axis=0, tiled=True)  13.7 us
    all_to_all x1, waiting for transfers between devices, shards(): lax.all_to_all(cotangent[0], 'ctx', split_axis=1, concat_axis=0, tiled=True)  13 us
    all_gather x1, blocking collectives, shards(): every = lax.all_gather(flat, 'ctx')  10.5 us
    all_to_all x1, starting transfers between devices, shards(): lax.all_to_all(features[0], 'ctx', split_axis=1, concat_axis=0, tiled=True)  5.33 us
    unnamed x19, local copies, waits for them, and re-layouts  5.01 us
  transfers between devices with their start and end apart: 4, of which 3 were waited for; matrix products, arithmetic and copies ran while one was open for 4% of the time, Pallas kernels for 0%

profile of v1, /device:TPU:0, one launch (start us, length us, event | category | flops | bytes accessed | tf_op | source)
XLA Modules:
  0.0 185.2 jit_solution(13631981334862379843)
XLA Ops:
  7.2 0.0 copy-start
  7.2 1.7 copy.33
  8.8 1.3 copy.23
  10.1 0.0 copy-start.2
  10.1 5.3 %all-to-all-start = ((bf16[128,8,512]{2,0,1:T(8,128)(2,1)}), bf16[128,8,512]{2,0,1:T(8,128)(2,1)S(1)}, u32[]{:S(2)}, u32[]{:S(2)}) async-start(bf16[128,8,512]{2,0,1:T(8,128)(2,1)} %copy.23), calls=%async_computation | async-start | bytes 2097152 | tf_op jit(solution)/shard_map/all_to_all | solution.py:158
  15.5 0.0 copy-done.2
  15.5 0.4 copy.34
  15.9 1.3 copy.24
  17.1 13.7 %all-to-all-done = bf16[128,8,512]{2,0,1:T(8,128)(2,1)S(1)} async-done(((bf16[128,8,512]{2,0,1:T(8,128)(2,1)}), bf16[128,8,512]{2,0,1:T(8,128)(2,1)S(1)}, u32[]{:S(2)}, u32[]{:S(2)}) %all-to-all-start) | async-done | bytes 1048608 | tf_op jit(solution)/shard_map/all_to_all | solution.py:158
  30.8 3.6 %all-to-all-start.1 = ((bf16[128,8,512]{2,0,1:T(8,128)(2,1)}), bf16[128,8,512]{2,0,1:T(8,128)(2,1)S(1)}, u32[]{:S(2)}, u32[]{:S(2)}) async-start(bf16[128,8,512]{2,0,1:T(8,128)(2,1)} %copy.24), calls=%async_computation.1 | async-start | bytes 2097152 | tf_op jit(solution)/shard_map/all_to_all | solution.py:159
  34.4 0.0 copy-done
  34.4 0.0 copy-start.3
  34.4 0.1 constant_dynamic-slice_fusion
  34.5 0.1 copy.32
  34.6 0.7 copy-done.3
  35.3 0.1 reshape.44
  35.4 0.0 copy-start.5
  35.5 0.1 copy.31
  35.6 0.5 copy-done.5
  36.1 0.0 copy-start.4
  36.1 0.1 iota_compare_fusion
  36.3 0.4 copy-done.4
  36.7 13.0 %all-to-all-done.1 = bf16[128,8,512]{2,0,1:T(8,128)(2,1)S(1)} async-done(((bf16[128,8,512]{2,0,1:T(8,128)(2,1)}), bf16[128,8,512]{2,0,1:T(8,128)(2,1)S(1)}, u32[]{:S(2)}, u32[]{:S(2)}) %all-to-all-start.1) | async-done | bytes 1048608 | tf_op jit(solution)/shard_map/all_to_all | solution.py:159
  49.7 50.7 %shard_map.84 = (bf16[1024,512]{1,0:T(8,128)(2,1)S(1)}, bf16[1024,512]{1,0:T(8,128)(2,1)S(1)}, f32[32,512]{1,0:T(8,128)S(1)}, f32[16,512]{1,0:T(8,128)S(1)}) custom-call(bf16[1024,512]{1,0:T(8,128)(2,1)S(1)} %bitcast.31, bf16[1024,512]{1,0:T(8,128)(2,1)S(1)} %bitcast.32, f32[512,9]{1,0:T(8,128)S(1)} %bitcast.33, f32[32,512]{1,0:T(8,128)S(1)} %convert_bitcast_fusion.taps), custom_call_target="tpu_custom_call" | custom-call | tf_op jit(solution)/shard_map/pallas_call | solution.py:168
  100.4 0.0 copy-start.1
  100.4 17.8 %all_to_all.70 = bf16[8,128,512]{2,1,0:T(8,128)(2,1)S(1)} all-to-all(bf16[8,128,512]{2,1,0:T(8,128)(2,1)S(1)} %bitcast.35), channel_id=1, replica_groups=mesh['dp'=4,'ctx'=8] {'ctx'}, dimensions={0} | all-to-all | bytes 2097152 | tf_op jit(solution)/shard_map/all_to_all | solution.py:198
  118.2 0.0 copy-done.1
  118.2 3.6 %all-to-all-start.2 = ((bf16[8,128,512]{2,1,0:T(8,128)(2,1)}), bf16[8,128,512]{2,1,0:T(8,128)(2,1)S(1)}, u32[]{:S(2)}, u32[]{:S(2)}) async-start(bf16[8,128,512]{2,1,0:T(8,128)(2,1)} %bitcast.34), calls=%async_computation.2 | async-start | bytes 2097152 | tf_op jit(solution)/shard_map/all_to_all | solution.py:197
  121.7 0.0 all-reduce.2.cloned.1.call-start
  121.8 0.7 all_gather.6
  122.5 0.0 all-reduce.2.cloned.1.call-update
  122.6 38.8 %all-reduce.2.cloned.1.call-done = f32[1,20992]{1,0:T(1,128)} async-done(((f32[1,20992]{1,0:T(1,128)}), f32[1,20992]{1,0:T(1,128)}) %all-reduce.2.cloned.1.call-update) | async-done | bytes 83984 | tf_op jit(solution)/shard_map/psum | solution.py:200
  161.3 10.5 %all-gather = f32[8,1,20992]{2,1,0:T(1,128)S(1)} all-gather(f32[1,1,20992]{2,1,0:T(1,128)} %bitcast.48), channel_id=1, replica_groups=mesh['dp'=4,'ctx'=8] {'ctx'}, dimensions={0}, use_global_device_ids=true | all-gather | bytes 755712 | tf_op jit(solution)/shard_map/all_gather | solution.py:201
  171.9 0.1 reshape.47
  172.0 0.8 bitcast_select_fusion
  172.8 1.0 copy.29
  173.8 0.8 reshape.49
  174.6 0.6 copy.28
  175.2 1.3 broadcast_in_dim.17
  176.5 0.0 all-to-all-done.2
  176.5 0.6 copy.27
  177.1 1.3 broadcast_in_dim.16
  (9 shorter events, 0.1 us)
Async XLA Ops:
  7.2 27.2 %copy-start = (bf16[512,256]{1,0:T(8,128)(2,1)S(1)}, bf16[512,256]{1,0:T(8,128)(2,1)}, u32[]{:S(2)}) copy-start(bf16[512,256]{1,0:T(8,128)(2,1)} %param.7) | copy-start | bytes 786436
  10.1 5.3 %copy-start.2 = (bf16[1,128,4096]{2,1,0:T(8,128)(2,1)S(1)}, bf16[1,128,4096]{2,1,0:T(8,128)(2,1)}, u32[]{:S(2)}) copy-start(bf16[1,128,4096]{2,1,0:T(8,128)(2,1)} %param.9) | copy-start | bytes 3145732
  10.1 20.7 %all-to-all-start = ((bf16[128,8,512]{2,0,1:T(8,128)(2,1)}), bf16[128,8,512]{2,0,1:T(8,128)(2,1)S(1)}, u32[]{:S(2)}, u32[]{:S(2)}) async-start(bf16[128,8,512]{2,0,1:T(8,128)(2,1)} %copy.23), calls=%async_computation | async-start | bytes 2097152 | tf_op jit(solution)/shard_map/all_to_all | solution.py:158
  30.8 18.9 %all-to-all-start.1 = ((bf16[128,8,512]{2,0,1:T(8,128)(2,1)}), bf16[128,8,512]{2,0,1:T(8,128)(2,1)S(1)}, u32[]{:S(2)}, u32[]{:S(2)}) async-start(bf16[128,8,512]{2,0,1:T(8,128)(2,1)} %copy.24), calls=%async_computation.1 | async-start | bytes 2097152 | tf_op jit(solution)/shard_map/all_to_all | solution.py:159
  34.4 0.9 copy-start.3
  35.4 0.7 copy-start.5
  36.1 0.6 copy-start.4
  100.4 17.8 %copy-start.1 = (bf16[1024,512]{1,0:T(8,128)(2,1)}, bf16[1024,512]{1,0:T(8,128)(2,1)S(1)}, u32[]{:S(2)}) copy-start(bf16[1024,512]{1,0:T(8,128)(2,1)S(1)} %get-tuple-element.8) | copy-start | bytes 3145732
  118.2 58.3 %all-to-all-start.2 = ((bf16[8,128,512]{2,1,0:T(8,128)(2,1)}), bf16[8,128,512]{2,1,0:T(8,128)(2,1)S(1)}, u32[]{:S(2)}, u32[]{:S(2)}) async-start(bf16[8,128,512]{2,1,0:T(8,128)(2,1)} %bitcast.34), calls=%async_computation.2 | async-start | bytes 2097152 | tf_op jit(solution)/shard_map/all_to_all | solution.py:197
  121.7 39.6 %all-reduce.2.cloned.1.call-start = ((), (), s32[]{:S(2)}) async-start(), calls=%async_computation.4 | async-start | bytes 167936 | tf_op jit(solution)/shard_map/psum | solution.py:200
Sparse Core Ops, SparseCore 0:
  125.5 35.8 all-reduce.1

commit v2 on v1

v2 whole, which is shorter than its diff:
```python
import functools

import jax
import jax.numpy as jnp
from jax import lax
from jax.experimental import pallas as pl
from jax.experimental.pallas import tpu as pltpu
from jax.sharding import PartitionSpec as P

PANEL = 128
UNIT = 16
TILE = 128
TAPS = 3
UNROLL = 2
MESH = pl.DeviceIdType.MESH


def rows_down(x, rows):
    return jnp.concatenate([jnp.zeros((rows, x.shape[1]), x.dtype), x[:-rows]], axis=0)


def rows_up(x, rows):
    return jnp.concatenate([x[rows:], jnp.zeros((rows, x.shape[1]), x.dtype)], axis=0)


def toeplitz(taps):
    width = taps.shape[1]
    x = jnp.broadcast_to(taps, (8, width))
    row = lax.broadcasted_iota(jnp.int32, (8, width), 0)
    for bit in (1, 2, 4):
        x = jnp.where((row & bit) != 0, pltpu.roll(x, bit, 1), x)
    rows = 8
    while rows < PANEL:
        x = jnp.concatenate([x, pltpu.roll(x, rows, 1)], axis=0)
        rows *= 2
    return x


def causal():
    shape = (PANEL, PANEL)
    return lax.broadcasted_iota(jnp.int32, shape, 1) >= lax.broadcasted_iota(jnp.int32, shape, 0)


def lag_sums(products):
    width = products.shape[1]
    first = jnp.where(causal(), products[:, :PANEL], 0.0)
    x = jnp.concatenate([first, products[:, PANEL:]], axis=1)
    rows = PANEL // 2
    while rows >= 8:
        x = x[:rows] + pltpu.roll(x[rows:], width - rows, 1)
        rows //= 2
    for step in (4, 2, 1):
        x = x + pltpu.roll(pltpu.roll(x, 8 - step, 0), width - step, 1)
    return x[0:1]


def tile_terms(reach, panels, ft, ct, wt, taps, out_t, in_t, fg, sg_t):
    rows = panels * UNIT

    def group(g, carry):
        first = pl.multiple_of(g * UNIT, UNIT)
        lane = lax.broadcasted_iota(jnp.int32, (rows, PANEL), 1)
        chan = pl.ds(first, UNIT)
        feat = ft[:, chan, :].reshape(rows, PANEL)
        cot = ct[:, chan, :].reshape(rows, PANEL)
        w_all = wt[chan, :]

        def weigh(k, x):
            w = jnp.broadcast_to(w_all[:, k : k + 1], (UNIT, PANEL))
            return (x.reshape(panels, UNIT, PANEL) * w[None]).reshape(rows, PANEL)

        feats = [feat]
        for tap in range(1, TAPS):
            turned = pltpu.roll(feat, tap, 1)
            feats.append(jnp.where(lane < tap, rows_down(turned, UNIT), turned))
        streams = []
        for m in range(3):
            total = weigh(m * TAPS, feats[0])
            for tap in range(1, TAPS):
                total = total + weigh(m * TAPS + tap, feats[tap])
            streams.append(total)
        query, key, value = streams
        mixed = (key * value).astype(jnp.bfloat16)
        grad_conv = (cot * query).astype(jnp.bfloat16)
        earlier = jnp.concatenate(
            [mixed] + [rows_down(mixed, o * UNIT) for o in range(1, reach)], axis=1
        )
        later = jnp.concatenate(
            [grad_conv] + [rows_up(grad_conv, o * UNIT) for o in range(1, reach)], axis=1
        )
        spread = toeplitz(taps[pl.ds(g, 1), :])
        spread = jnp.concatenate(
            [jnp.where(causal(), spread[:, :PANEL], 0.0), spread[:, PANEL:]], axis=1
        ).astype(jnp.bfloat16)
        stacked = jnp.concatenate(
            [spread[:, o * PANEL : (o + 1) * PANEL] for o in range(reach)], axis=0
        )
        conv = jnp.dot(earlier, stacked, preferred_element_type=jnp.float32)
        back = lax.dot_general(
            later, spread, (((1,), (1,)), ((), ())), preferred_element_type=jnp.float32
        )
        products = lax.dot_general(
            mixed, later, (((0,), (0,)), ((), ())), preferred_element_type=jnp.float32
        )
        fg[pl.ds(g, 1), :] = lag_sums(products)
        out_t[:, chan, :] = (query * conv).reshape(panels, UNIT, PANEL)
        grads = (cot * conv, back * value, back * key)
        grad_in = None
        for tap in range(TAPS):
            part = weigh(tap, grads[0]) + weigh(TAPS + tap, grads[1]) + weigh(2 * TAPS + tap, grads[2])
            if tap:
                turned = pltpu.roll(part, PANEL - tap, 1)
                part = jnp.where(lane >= PANEL - tap, rows_up(turned, UNIT), turned)
            grad_in = part if grad_in is None else grad_in + part
        in_t[:, chan, :] = grad_in.reshape(panels, UNIT, PANEL)
        small_lane = lax.broadcasted_iota(jnp.int32, (UNIT, PANEL), 1)
        sums = jnp.zeros((UNIT, PANEL), jnp.float32)
        for m in range(3):
            for tap in range(TAPS):
                part = jnp.sum((grads[m] * feats[tap]).reshape(panels, UNIT, PANEL), axis=0)
                sums = jnp.where(small_lane == m * TAPS + tap, jnp.sum(part, axis=1, keepdims=True), sums)
        sg_t[chan, :] = sums
        return carry

    lax.fori_loop(0, TILE // UNIT, group, 0, unroll=UNROLL)


def layer_kernel(
    reach, ndp, nctx, f_hbm, c_hbm, wt, taps, out_hbm, in_hbm, all_hbm,
    arrived, leaving, ft, ct, out_t, in_t, fg, sg_t, pay, parts, sums,
    own_sem, in_send, in_recv, out_send, out_recv, keep_sem,
    rs_send, rs_recv, gd_send, gd_recv, gd_own, gc_send, gc_recv,
):
    dp, me = lax.axis_index("dp"), lax.axis_index("ctx")
    width = arrived.shape[3]
    tiles = width // TILE
    chunk = sums.shape[1]
    ins, outs = (f_hbm, c_hbm), (out_hbm, in_hbm)

    def ctx_peer(k):
        return lax.rem(me + k, nctx)

    def dp_peer(k):
        return lax.rem(dp + k, ndp)

    def lanes(j):
        return pl.ds(pl.multiple_of(j * TILE, TILE), TILE)

    def cols(owner, j):
        return pl.ds(pl.multiple_of(owner * width + j * TILE, TILE), TILE)

    def copy(src, dst, send, recv, device):
        return pltpu.make_async_remote_copy(
            src_ref=src, dst_ref=dst, send_sem=send, recv_sem=recv, device_id=device, device_id_type=MESH
        )

    def in_copy(a, j, k, slot):
        return copy(
            ins[a].at[:, cols(ctx_peer(k), j)],
            arrived.at[a, slot, :, lanes(j)],
            in_send.at[a, j, k],
            in_recv.at[a, j, k],
            (dp, ctx_peer(k)),
        )

    def in_own(a, j):
        return pltpu.make_async_copy(
            ins[a].at[:, cols(me, j)], arrived.at[a, me, :, lanes(j)], own_sem.at[a, j]
        )

    def out_copy(a, j, k, slot):
        return copy(
            leaving.at[a, ctx_peer(k), :, lanes(j)],
            outs[a].at[:, cols(slot, j)],
            out_send.at[a, j, k],
            out_recv.at[a, j, k],
            (dp, ctx_peer(k)),
        )

    def out_own(a, j):
        return pltpu.make_async_copy(
            leaving.at[a, me, :, lanes(j)], outs[a].at[:, cols(me, j)], keep_sem.at[a, j]
        )

    def rs_copy(j, k):
        return copy(
            pay.at[j, dp_peer(k)], parts.at[j, k], rs_send.at[j, k], rs_recv.at[j, k], (dp_peer(k), me)
        )

    def gd_copy(j, k, slot):
        return copy(
            sums.at[j], all_hbm.at[me, j, slot], gd_send.at[j, k], gd_recv.at[j, k], (dp_peer(k), me)
        )

    def gd_keep(j):
        return pltpu.make_async_copy(sums.at[j], all_hbm.at[me, j, dp], gd_own.at[j])

    def gc_copy(j, k, slot):
        return copy(
            all_hbm.at[me, j], all_hbm.at[slot, j], gc_send.at[j, k], gc_recv.at[j, k], (dp, ctx_peer(k))
        )

    def each(count, body):
        def step(i, carry):
            body(i)
            return carry

        lax.fori_loop(0, count, step, 0)

    barrier = pltpu.get_barrier_semaphore()
    for k in range(1, nctx):
        pl.semaphore_signal(barrier, inc=1, device_id=(dp, ctx_peer(k)), device_id_type=MESH)
    for k in range(1, ndp):
        pl.semaphore_signal(barrier, inc=1, device_id=(dp_peer(k), me), device_id_type=MESH)
    for a in range(2):
        each(tiles, lambda j: in_own(a, j).start())
    pl.semaphore_wait(barrier, nctx + ndp - 2)

    def send_in(j):
        for a in range(2):
            each(nctx - 1, lambda i: in_copy(a, j, i + 1, me).start())

    each(tiles, send_in)

    def spread_dp(j):
        each(ndp - 1, lambda i: rs_copy(j, i + 1).wait_recv())
        total = pay[j, dp]
        for k in range(1, ndp):
            total = total + parts[j, k]
        sums[j] = total
        gd_keep(j).start()
        each(ndp - 1, lambda i: gd_copy(j, i + 1, dp).start())

    def spread_ctx(j):
        gd_keep(j).wait()
        each(ndp - 1, lambda i: gd_copy(j, i + 1, lax.rem(dp + ndp - i - 1, ndp)).wait_recv())
        each(nctx - 1, lambda i: gc_copy(j, i + 1, me).start())

    def one_tile(j):
        for a in range(2):
            in_own(a, j).wait()
            each(
                nctx - 1,
                lambda i: in_copy(a, j, i + 1, lax.rem(me + nctx - i - 1, nctx)).wait_recv(),
            )

        def turn_in(n):
            ft[n] = arrived[0, n, :, lanes(j)].astype(jnp.float32).T
            ct[n] = arrived[1, n, :, lanes(j)].astype(jnp.float32).T

        each(nctx, turn_in)
        units = TILE // UNIT
        tile_terms(
            reach, nctx, ft, ct, wt.at[lanes(j), :],
            taps.at[pl.ds(pl.multiple_of(j * units, units), units), :], out_t, in_t, fg, sg_t,
        )

        def turn_out(n):
            leaving[0, n, :, lanes(j)] = out_t[n].T.astype(jnp.bfloat16)
            leaving[1, n, :, lanes(j)] = in_t[n].T.astype(jnp.bfloat16)

        each(nctx, turn_out)
        rows = [fg[:, o * PANEL : (o + 1) * PANEL] for o in range(reach)] + [sg_t[...].T[:UNIT]]
        filled = reach * units + UNIT
        if filled < ndp * chunk:
            rows.append(jnp.zeros((ndp * chunk - filled, PANEL), jnp.float32))
        pay[j] = jnp.concatenate(rows, axis=0).reshape(ndp, chunk, PANEL)
        each(ndp - 1, lambda i: rs_copy(j, i + 1).start())
        for a in range(2):
            out_own(a, j).start()
            each(nctx - 1, lambda i: out_copy(a, j, i + 1, me).start())

        @pl.when(j >= 1)
        def _():
            spread_dp(j - 1)

        @pl.when(j >= 2)
        def _():
            spread_ctx(j - 2)

    each(tiles, one_tile)
    if tiles >= 2:
        spread_ctx(tiles - 2)
    spread_dp(tiles - 1)
    spread_ctx(tiles - 1)

    def finish(j):
        for a in range(2):
            each(nctx - 1, lambda i: in_copy(a, j, i + 1, me).wait_send())
            out_own(a, j).wait()
            each(nctx - 1, lambda i: out_copy(a, j, i + 1, me).wait_send())
            each(
                nctx - 1,
                lambda i: out_copy(a, j, i + 1, lax.rem(me + nctx - i - 1, nctx)).wait_recv(),
            )
        each(ndp - 1, lambda i: rs_copy(j, i + 1).wait_send())
        each(ndp - 1, lambda i: gd_copy(j, i + 1, dp).wait_send())
        each(nctx - 1, lambda i: gc_copy(j, i + 1, me).wait_send())
        each(nctx - 1, lambda i: gc_copy(j, i + 1, lax.rem(me + nctx - i - 1, nctx)).wait_recv())

    each(tiles, finish)


def shards(ndp, nctx, features, short_weights, filters, reach_panels, cotangent):
    filter_len, groups = filters.shape
    channels = features.shape[2]
    reach = filter_len // PANEL
    lag_pos = lax.broadcasted_iota(jnp.int32, (filter_len, groups), 0)
    keep = lag_pos < reach_panels[None, :] * PANEL
    masked = jnp.where(keep, filters, jnp.zeros((), filters.dtype))
    rows = features.shape[1]
    assert rows == PANEL and features.shape[0] == 1
    width = channels // nctx
    tiles = width // TILE
    me = lax.axis_index("ctx")
    units = width // UNIT
    tile_units = TILE // UNIT
    taps = lax.dynamic_slice_in_dim(masked, me * units, units, 1).T.astype(jnp.float32)
    wt = lax.dynamic_slice_in_dim(short_weights.reshape(9, channels), me * width, width, 1).T
    filled = reach * tile_units + UNIT
    chunk = -(-filled // (8 * ndp)) * 8
    hbm = pl.BlockSpec(memory_space=pl.ANY)
    vmem = pl.BlockSpec(memory_space=pltpu.VMEM)
    dma = pltpu.SemaphoreType.DMA
    turned = pltpu.VMEM((nctx, TILE, PANEL), jnp.float32)
    layer_out, input_grad, every = pl.pallas_call(
        functools.partial(layer_kernel, reach, ndp, nctx),
        in_specs=[hbm, hbm, vmem, vmem],
        out_specs=[hbm, hbm, hbm],
        out_shape=[
            jax.ShapeDtypeStruct((rows, channels), jnp.bfloat16),
            jax.ShapeDtypeStruct((rows, channels), jnp.bfloat16),
            jax.ShapeDtypeStruct((nctx, tiles, ndp, chunk, PANEL), jnp.float32),
        ],
        scratch_shapes=[
            pltpu.VMEM((2, nctx, PANEL, width), jnp.bfloat16),
            pltpu.VMEM((2, nctx, PANEL, width), jnp.bfloat16),
            turned,
            turned,
            turned,
            turned,
            pltpu.VMEM((tile_units, filter_len), jnp.float32),
            pltpu.VMEM((TILE, PANEL), jnp.float32),
            pltpu.VMEM((tiles, ndp, chunk, PANEL), jnp.float32),
            pltpu.VMEM((tiles, ndp, chunk, PANEL), jnp.float32),
            pltpu.VMEM((tiles, chunk, PANEL), jnp.float32),
            dma((2, tiles)),
            dma((2, tiles, nctx)),
            dma((2, tiles, nctx)),
            dma((2, tiles, nctx)),
            dma((2, tiles, nctx)),
            dma((2, tiles)),
            dma((tiles, ndp)),
            dma((tiles, ndp)),
            dma((tiles, ndp)),
            dma((tiles, ndp)),
            dma((tiles,)),
            dma((tiles, nctx)),
            dma((tiles, nctx)),
        ],
        compiler_params=pltpu.CompilerParams(
            collective_id=0, has_side_effects=True, vmem_limit_bytes=48 * 2**20
        ),
    )(features[0], cotangent[0], wt, taps)
    every = every.reshape(nctx, tiles, ndp * chunk, PANEL)
    lag_rows = every[:, :, : reach * tile_units].reshape(nctx, tiles, reach, tile_units, PANEL)
    filter_sum = lag_rows.transpose(2, 4, 0, 1, 3).reshape(filter_len, groups)
    filter_grad = jnp.where(keep, filter_sum, jnp.zeros((), jnp.float32))
    short_rows = every[:, :, reach * tile_units : reach * tile_units + 9]
    short_grad = short_rows.transpose(2, 0, 1, 3).reshape(3, 3, channels)
    return (layer_out[None], input_grad[None], filter_grad, short_grad)


def solution(mesh):
    return jax.shard_map(
        functools.partial(shards, mesh.shape["dp"], mesh.shape["ctx"]),
        mesh=mesh,
        in_specs=(P("dp", "ctx", None), P(), P(), P(), P("dp", "ctx", None)),
        out_specs=(P("dp", "ctx", None), P("dp", "ctx", None), P(), P()),
        check_vma=False,
    )
```

time: 186 us -> 76.9 us (0.41)
  waiting for transfers between devices: 65.5 us -> 0 us
  blocking collectives: 28.2 us -> 0 us
  Pallas kernels: 50.7 us -> 67.5 us
  between operations: 14.2 us -> 0.78 us
  starting transfers between devices: 12.5 us -> 0 us
  local copies, waits for them, and re-layouts: 13.2 us -> 7.38 us
    psum x1 -> x0, waiting for transfers between devices: 38.8 us -> none  [shards(): flat = lax.psum(flat, 'dp')]
    all_to_all x3 -> x0, waiting for transfers between devices: 26.7 us -> none  [the longest x1 13.7 us: shards(): lax.all_to_all(features[0], 'ctx', split_axis=1, concat_axis=0, tiled=True)]
    all_to_all x1 -> x0, blocking collectives: 17.8 us -> none  [shards(): lax.all_to_all(in_local, 'ctx', split_axis=0, concat_axis=1, tiled=True)]
    pallas_call x1, Pallas kernels: 50.7 us -> 67.5 us  [shards(): pl.pallas_call(functools.partial(layer_kernel, reach, ndp, nctx), in_spec...]
    all_to_all x3 -> x0, starting transfers between devices: 12.4 us -> none  [the longest x1 5.33 us: shards(): lax.all_to_all(features[0], 'ctx', split_axis=1, concat_axis=0, tiled=True)]
    all_gather x1 -> x0, blocking collectives: 10.5 us -> none  [shards(): every = lax.all_gather(flat, 'ctx')]
    all_to_all x4 -> x0, local copies, waits for them, and re-layouts: 3.72 us -> none  [the longest x1 1.28 us: shards(): lax.all_to_all(cotangent[0], 'ctx', split_axis=1, concat_axis=0, tiled=True)]
    broadcast_in_dim x2 -> x0, local copies, waits for them, and re-layouts: 2.62 us -> none  [the longest x1 1.31 us: shards(): lax.all_to_all(in_local, 'ctx', split_axis=0, concat_axis=1, tiled=True)]
  transfers between devices with their start and end apart: 4 -> 0, of which waited for: 3 -> 0; matrix products, arithmetic and copies ran while one was open for 4% -> 0% of each run, Pallas kernels for 0% -> 0%
where the time goes in v2:
time: 76.9 us; the launch traced here: 76.7 us
  Pallas kernels  67.5 us (88%)
  local copies, waits for them, and re-layouts  7.38 us (10%)
  other arithmetic  1.04 us (1%)
  between operations  0.78 us (1%)
    pallas_call x1, Pallas kernels, shards(): pl.pallas_call(functools.partial(layer_kernel, reach, ndp, nctx), in_spec...  67.5 us
    unnamed x15, local copies, waits for them, and re-layouts  5.36 us

profile of v2, /device:TPU:0, one launch (start us, length us, event | category | flops | bytes accessed | tf_op | source)
XLA Modules:
  0.0 76.7 jit_solution(17977544615137316007)
XLA Ops:
  0.6 0.0 copy-start
  0.6 0.0 copy-start.1
  0.7 0.8 %broadcast_multiply_fusion = s32[256]{0:T(256)S(1)} fusion(s32[256]{0:T(256)} %param.8), kind=kLoop, calls=%fused_computation.7 | loop fusion | flops 256 | bytes 2048 | tf_op jit(solution)/shard_map/mul | solution.py:309
  1.4 0.1 iota_compare_fusion
  1.6 0.0 copy-done
  1.6 0.1 constant_dynamic-slice_fusion
  1.7 0.1 copy.18
  1.8 1.0 %reshape.25 = f32[9,4096]{1,0:T(8,128)S(1)} reshape(f32[3,3,4096]{2,1,0:T(4,128)} %param.6) | data formatting | bytes 294912 | tf_op jit(solution)/shard_map/reshape | solution.py:319
  2.9 0.1 copy.17
  3.0 0.0 copy-done.1
  3.0 0.0 copy-start.2
  3.0 1.2 %copy-done.2 = bf16[1,128,4096]{2,1,0:T(8,128)(2,1)S(1)} copy-done((bf16[1,128,4096]{2,1,0:T(8,128)(2,1)S(1)}, bf16[1,128,4096]{2,1,0:T(8,128)(2,1)}, u32[]{:S(2)}) %copy-start.2) | copy-done | bytes 1048600
  4.2 67.5 %shard_map.84 = (bf16[128,4096]{1,0:T(8,128)(2,1)S(1)}, bf16[128,4096]{1,0:T(8,128)(2,1)S(1)}, f32[8,4,4,16,128]{4,3,2,1,0:T(8,128)S(1)}) custom-call(bf16[128,4096]{1,0:T(8,128)(2,1)S(1)} %bitcast.15, bf16[128,4096]{1,0:T(8,128)(2,1)S(1)} %bitcast.16, f32[512,9]{1,0:T(8,128)S(1)} %bitcast.17, f32[32,512]{1,0:T(8,128)S(1)} %convert_bitcast_fusion.taps), custom_call_target="tpu_custom_call" | custom-call | tf_op jit(solution)/shard_map/pallas_call | solution.py:326
  71.8 0.0 copy-start.3
  71.8 1.0 %copy-done.3 = bf16[128,4096]{1,0:T(8,128)(2,1)} copy-done((bf16[128,4096]{1,0:T(8,128)(2,1)}, bf16[128,4096]{1,0:T(8,128)(2,1)S(1)}, u32[]{:S(2)}) %copy-start.3) | copy-done | bytes 1048600
  72.8 0.1 copy.15
  72.9 0.0 copy-start.4
  72.9 0.1 broadcast_select_fusion
  73.0 1.0 %copy.16 = f32[512,256]{1,0:T(8,128)} copy(f32[512,256]{0,1:T(8,128)S(1)} %broadcast_select_fusion) | data formatting | bytes 1048576
  74.0 0.8 %reshape.29 = f32[3,3,4096]{2,1,0:T(4,128)} reshape(f32[9,8,4,128]{3,2,1,0:T(4,128)S(1)} %copy.15) | data formatting | bytes 294912 | tf_op jit(solution)/shard_map/reshape | solution.py:370
  74.8 0.0 copy-done.4
  74.8 1.0 %copy.21 = bf16[1,128,4096]{2,1,0:T(8,128)(2,1)} copy(bf16[1,128,4096]{2,1,0:T(8,128)(2,1)S(1)} %bitcast.19) | data formatting | bytes 2097152
  75.8 1.0 %copy.22 = bf16[1,128,4096]{2,1,0:T(8,128)(2,1)} copy(bf16[1,128,4096]{2,1,0:T(8,128)(2,1)S(1)} %bitcast.18) | data formatting | bytes 2097152
  (4 shorter events, 0.1 us)
Async XLA Ops:
  0.6 1.0 %copy-start = (bf16[512,256]{1,0:T(8,128)(2,1)S(1)}, bf16[512,256]{1,0:T(8,128)(2,1)}, u32[]{:S(2)}) copy-start(bf16[512,256]{1,0:T(8,128)(2,1)} %param.7) | copy-start | bytes 786436
  0.6 2.4 %copy-start.1 = (bf16[1,128,4096]{2,1,0:T(8,128)(2,1)S(1)}, bf16[1,128,4096]{2,1,0:T(8,128)(2,1)}, u32[]{:S(2)}) copy-start(bf16[1,128,4096]{2,1,0:T(8,128)(2,1)} %param.5) | copy-start | bytes 3145732
  3.0 1.2 %copy-start.2 = (bf16[1,128,4096]{2,1,0:T(8,128)(2,1)S(1)}, bf16[1,128,4096]{2,1,0:T(8,128)(2,1)}, u32[]{:S(2)}) copy-start(bf16[1,128,4096]{2,1,0:T(8,128)(2,1)} %param.9) | copy-start | bytes 3145732
  71.8 1.0 %copy-start.3 = (bf16[128,4096]{1,0:T(8,128)(2,1)}, bf16[128,4096]{1,0:T(8,128)(2,1)S(1)}, u32[]{:S(2)}) copy-start(bf16[128,4096]{1,0:T(8,128)(2,1)S(1)} %get-tuple-element.7) | copy-start | bytes 3145732
  72.9 1.9 %copy-start.4 = (bf16[128,4096]{1,0:T(8,128)(2,1)S(1)}, bf16[128,4096]{1,0:T(8,128)(2,1)}, u32[]{:S(2)}) copy-start(bf16[128,4096]{1,0:T(8,128)(2,1)} %copy-done.3) | copy-start | bytes 3145732

commit v3 on v2

--- a/solution.py
+++ b/solution.py
@@ -11,7 +11,7 @@
 UNIT = 16
 TILE = 128
 TAPS = 3
-UNROLL = 2
+UNROLL = 4
 MESH = pl.DeviceIdType.MESH
 
 
@@ -21,6 +21,11 @@
 
 def rows_up(x, rows):
     return jnp.concatenate([x[rows:], jnp.zeros((rows, x.shape[1]), x.dtype)], axis=0)
+
+
+def causal():
+    shape = (PANEL, PANEL)
+    return lax.broadcasted_iota(jnp.int32, shape, 1) >= lax.broadcasted_iota(jnp.int32, shape, 0)
 
 
 def toeplitz(taps):
@@ -33,12 +38,8 @@
     while rows < PANEL:
         x = jnp.concatenate([x, pltpu.roll(x, rows, 1)], axis=0)
         rows *= 2
-    return x
-
-
-def causal():
-    shape = (PANEL, PANEL)
-    return lax.broadcasted_iota(jnp.int32, shape, 1) >= lax.broadcasted_iota(jnp.int32, shape, 0)
+    first = jnp.where(causal(), x[:, :PANEL], 0.0)
+    return jnp.concatenate([first, x[:, PANEL:]], axis=1).astype(jnp.bfloat16)
 
 
 def lag_sums(products):
@@ -54,7 +55,7 @@
     return x[0:1]
 
 
-def tile_terms(reach, panels, ft, ct, wt, taps, out_t, in_t, fg, sg_t):
+def tile_terms(reach, panels, ft, ct, wt, spreads, out_t, in_t, fg, sg_t):
     rows = panels * UNIT
 
     def group(g, carry):
@@ -88,10 +89,7 @@
         later = jnp.concatenate(
             [grad_conv] + [rows_up(grad_conv, o * UNIT) for o in range(1, reach)], axis=1
         )
-        spread = toeplitz(taps[pl.ds(g, 1), :])
-        spread = jnp.concatenate(
-            [jnp.where(causal(), spread[:, :PANEL], 0.0), spread[:, PANEL:]], axis=1
-        ).astype(jnp.bfloat16)
+        spread = spreads[g]
         stacked = jnp.concatenate(
             [spread[:, o * PANEL : (o + 1) * PANEL] for o in range(reach)], axis=0
         )
@@ -127,7 +125,7 @@
 
 def layer_kernel(
     reach, ndp, nctx, f_hbm, c_hbm, wt, taps, out_hbm, in_hbm, all_hbm,
-    arrived, leaving, ft, ct, out_t, in_t, fg, sg_t, pay, parts, sums,
+    arrived, leaving, spreads, ft, ct, out_t, in_t, fg, sg_t, pay, parts, sums,
     own_sem, in_send, in_recv, out_send, out_recv, keep_sem,
     rs_send, rs_recv, gd_send, gd_recv, gd_own, gc_send, gc_recv,
 ):
@@ -200,12 +198,12 @@
             all_hbm.at[me, j], all_hbm.at[slot, j], gc_send.at[j, k], gc_recv.at[j, k], (dp, ctx_peer(k))
         )
 
-    def each(count, body):
+    def each(count, body, unroll=1):
         def step(i, carry):
             body(i)
             return carry
 
-        lax.fori_loop(0, count, step, 0)
+        lax.fori_loop(0, count, step, 0, unroll=unroll)
 
     barrier = pltpu.get_barrier_semaphore()
     for k in range(1, nctx):
@@ -222,6 +220,11 @@
 
     each(tiles, send_in)
 
+    def build(g):
+        spreads[g] = toeplitz(taps[pl.ds(g, 1), :])
+
+    each(taps.shape[0], build, UNROLL)
+
     def spread_dp(j):
         each(ndp - 1, lambda i: rs_copy(j, i + 1).wait_recv())
         total = pay[j, dp]
@@ -248,18 +251,18 @@
             ft[n] = arrived[0, n, :, lanes(j)].astype(jnp.float32).T
             ct[n] = arrived[1, n, :, lanes(j)].astype(jnp.float32).T
 
-        each(nctx, turn_in)
+        each(nctx, turn_in, UNROLL)
         units = TILE // UNIT
         tile_terms(
             reach, nctx, ft, ct, wt.at[lanes(j), :],
-            taps.at[pl.ds(pl.multiple_of(j * units, units), units), :], out_t, in_t, fg, sg_t,
+            spreads.at[pl.ds(j * units, units)], out_t, in_t, fg, sg_t,
         )
 
         def turn_out(n):
             leaving[0, n, :, lanes(j)] = out_t[n].T.astype(jnp.bfloat16)
             leaving[1, n, :, lanes(j)] = in_t[n].T.astype(jnp.bfloat16)
 
-        each(nctx, turn_out)
+        each(nctx, turn_out, UNROLL)
         rows = [fg[:, o * PANEL : (o + 1) * PANEL] for o in range(reach)] + [sg_t[...].T[:UNIT]]
         filled = reach * units + UNIT
         if filled < ndp * chunk:
@@ -319,7 +322,7 @@
     wt = lax.dynamic_slice_in_dim(short_weights.reshape(9, channels), me * width, width, 1).T
     filled = reach * tile_units + UNIT
     chunk = -(-filled // (8 * ndp)) * 8
-    hbm = pl.BlockSpec(memory_space=pl.ANY)
+    hbm = pl.BlockSpec(memory_space=pltpu.HBM)
     vmem = pl.BlockSpec(memory_space=pltpu.VMEM)
     dma = pltpu.SemaphoreType.DMA
     turned = pltpu.VMEM((nctx, TILE, PANEL), jnp.float32)
@@ -335,6 +338,7 @@
         scratch_shapes=[
             pltpu.VMEM((2, nctx, PANEL, width), jnp.bfloat16),
             pltpu.VMEM((2, nctx, PANEL, width), jnp.bfloat16),
+            pltpu.VMEM((units, PANEL, filter_len), jnp.bfloat16),
             turned,
             turned,
             turned,
@@ -359,7 +363,7 @@
             dma((tiles, nctx)),
         ],
         compiler_params=pltpu.CompilerParams(
-            collective_id=0, has_side_effects=True, vmem_limit_bytes=48 * 2**20
+            collective_id=0, has_side_effects=True, vmem_limit_bytes=63 * 2**20
         ),
     )(features[0], cotangent[0], wt, taps)
     every = every.reshape(nctx, tiles, ndp * chunk, PANEL)

time: 76.9 us -> 78.5 us (1.021)
  local copies, waits for them, and re-layouts: 7.38 us -> 8.58 us
    slice x1, local copies, waits for them, and re-layouts: 0.04 us -> 1.09 us  [shards(): every[:, :, :reach * tile_units]]
    transpose x2, local copies, waits for them, and re-layouts: 0.08 us -> 1.04 us  [shards(): short_grad = short_rows.transpose(2, 0, 1, 3).reshape(3, 3, channels)]
    reshape x1, local copies, waits for them, and re-layouts: 1 us -> 0.07 us  [shards(): short_weights.reshape(9, channels)]
where the time goes in v3:
time: 78.5 us; the launch traced here: 78.2 us
  Pallas kernels  67.9 us (86%)
  local copies, waits for them, and re-layouts  8.58 us (11%)
  other arithmetic  0.89 us (1%)
    pallas_call x1, Pallas kernels, shards(): pl.pallas_call(functools.partial(layer_kernel, reach, ndp, nctx), in_spec...  67.9 us
    unnamed x15, local copies, waits for them, and re-layouts  5.49 us

profile of v3, /device:TPU:0, one launch (start us, length us, event | category | flops | bytes accessed | tf_op | source)
XLA Modules:
  0.0 78.2 jit_solution(3236416676740051008)
XLA Ops:
  0.6 0.0 copy-start
  0.7 0.0 copy-start.4
  0.7 0.7 copy-done.4
  1.4 0.1 iota_compare_fusion
  1.5 0.1 copy-done
  1.6 0.1 constant_dynamic-slice_fusion
  1.7 0.0 copy-start.3
  1.7 0.1 copy.18
  1.8 0.6 convert_bitcast_fusion.taps
  2.5 0.2 copy-done.3
  2.6 0.1 reshape.25
  2.7 0.9 %copy.17 = f32[9,512]{0,1:T(8,128)} copy(f32[9,512]{1,0:T(8,128)S(1)} %constant_dynamic-slice_fusion.1) | data formatting | bytes 36864
  3.6 67.9 %shard_map.84 = (bf16[128,4096]{1,0:T(8,128)(2,1)}, bf16[128,4096]{1,0:T(8,128)(2,1)}, f32[8,4,4,16,128]{4,3,2,1,0:T(8,128)}) custom-call(bf16[128,4096]{1,0:T(8,128)(2,1)} %bitcast.16, bf16[128,4096]{1,0:T(8,128)(2,1)} %bitcast.17, f32[512,9]{1,0:T(8,128)} %bitcast.18, f32[32,512]{1,0:T(8,128)} %convert_bitcast_fusion.taps), custom_call_target="tpu_custom_call" | custom-call | tf_op jit(solution)/shard_map/pallas_call | solution.py:329
  71.5 1.0 %slice_bitcast_fusion = f32[9,8,4,128]{3,0,2,1:T(8,128)S(1)} fusion(f32[8,4,64,128]{3,2,1,0:T(8,128)} %bitcast.21), kind=kLoop, calls=%fused_computation.1 | loop fusion | bytes 294912 | tf_op jit(solution)/shard_map/transpose | solution.py:374
  72.5 1.1 %slice.8 = f32[8,4,32,128]{3,2,1,0:T(8,128)S(1)} slice(f32[8,4,64,128]{3,2,1,0:T(8,128)} %bitcast.22), slice={[0:8], [0:4], [0:32], [0:128]} | slice | bytes 1048576 | tf_op jit(solution)/shard_map/slice | solution.py:370
  73.6 0.1 copy.15
  73.7 0.0 copy-start.2
  73.7 0.1 broadcast_select_fusion
  73.8 1.0 %copy.16 = f32[512,256]{1,0:T(8,128)} copy(f32[512,256]{0,1:T(8,128)S(1)} %broadcast_select_fusion) | data formatting | bytes 1048576
  74.8 0.8 reshape.29
  75.6 0.0 copy-done.2
  75.6 0.0 copy-start.1
  75.6 1.0 %copy.21 = bf16[1,128,4096]{2,1,0:T(8,128)(2,1)} copy(bf16[1,128,4096]{2,1,0:T(8,128)(2,1)S(1)} %bitcast.20) | data formatting | bytes 2097152
  76.6 0.6 copy-done.1
  77.2 1.0 %copy.22 = bf16[1,128,4096]{2,1,0:T(8,128)(2,1)} copy(bf16[1,128,4096]{2,1,0:T(8,128)(2,1)S(1)} %bitcast.19) | data formatting | bytes 2097152
  (2 shorter events, 0.0 us)
Async XLA Ops:
  0.6 1.0 %copy-start = (bf16[512,256]{1,0:T(8,128)(2,1)S(1)}, bf16[512,256]{1,0:T(8,128)(2,1)}, u32[]{:S(2)}) copy-start(bf16[512,256]{1,0:T(8,128)(2,1)} %param.7) | copy-start | bytes 786436
  0.7 0.7 copy-start.4
  1.7 0.9 %copy-start.3 = (f32[3,3,4096]{2,1,0:T(4,128)S(1)}, f32[3,3,4096]{2,1,0:T(4,128)}, u32[]{:S(2)}) copy-start(f32[3,3,4096]{2,1,0:T(4,128)} %param.6) | copy-start | bytes 442372
  73.7 1.9 %copy-start.2 = (bf16[128,4096]{1,0:T(8,128)(2,1)S(1)}, bf16[128,4096]{1,0:T(8,128)(2,1)}, u32[]{:S(2)}) copy-start(bf16[128,4096]{1,0:T(8,128)(2,1)} %get-tuple-element.7) | copy-start | bytes 3145732
  75.6 1.6 %copy-start.1 = (bf16[128,4096]{1,0:T(8,128)(2,1)S(1)}, bf16[128,4096]{1,0:T(8,128)(2,1)}, u32[]{:S(2)}) copy-start(bf16[128,4096]{1,0:T(8,128)(2,1)} %get-tuple-element.8) | copy-start | bytes 3145732

commit v4 on v3

--- a/solution.py
+++ b/solution.py
@@ -185,17 +185,17 @@
             pay.at[j, dp_peer(k)], parts.at[j, k], rs_send.at[j, k], rs_recv.at[j, k], (dp_peer(k), me)
         )
 
+    def gc_copy(j, k, slot):
+        return copy(
+            sums.at[j], all_hbm.at[j, dp, slot], gc_send.at[j, k], gc_recv.at[j, k], (dp, ctx_peer(k))
+        )
+
+    def gc_keep(j):
+        return pltpu.make_async_copy(sums.at[j], all_hbm.at[j, dp, me], gd_own.at[j])
+
     def gd_copy(j, k, slot):
         return copy(
-            sums.at[j], all_hbm.at[me, j, slot], gd_send.at[j, k], gd_recv.at[j, k], (dp_peer(k), me)
-        )
-
-    def gd_keep(j):
-        return pltpu.make_async_copy(sums.at[j], all_hbm.at[me, j, dp], gd_own.at[j])
-
-    def gc_copy(j, k, slot):
-        return copy(
-            all_hbm.at[me, j], all_hbm.at[slot, j], gc_send.at[j, k], gc_recv.at[j, k], (dp, ctx_peer(k))
+            all_hbm.at[j, dp], all_hbm.at[j, slot], gd_send.at[j, k], gd_recv.at[j, k], (dp_peer(k), me)
         )
 
     def each(count, body, unroll=1):
@@ -225,19 +225,19 @@
 
     each(taps.shape[0], build, UNROLL)
 
-    def spread_dp(j):
+    def spread_ctx(j):
         each(ndp - 1, lambda i: rs_copy(j, i + 1).wait_recv())
         total = pay[j, dp]
         for k in range(1, ndp):
             total = total + parts[j, k]
-        sums[j] = total
-        gd_keep(j).start()
+        sums[j] = total.astype(jnp.bfloat16)
+        gc_keep(j).start()
+        each(nctx - 1, lambda i: gc_copy(j, i + 1, me).start())
+
+    def spread_dp(j):
+        gc_keep(j).wait()
+        each(nctx - 1, lambda i: gc_copy(j, i + 1, lax.rem(me + nctx - i - 1, nctx)).wait_recv())
         each(ndp - 1, lambda i: gd_copy(j, i + 1, dp).start())
-
-    def spread_ctx(j):
-        gd_keep(j).wait()
-        each(ndp - 1, lambda i: gd_copy(j, i + 1, lax.rem(dp + ndp - i - 1, ndp)).wait_recv())
-        each(nctx - 1, lambda i: gc_copy(j, i + 1, me).start())
 
     def one_tile(j):
         for a in range(2):
@@ -275,17 +275,17 @@
 
         @pl.when(j >= 1)
         def _():
-            spread_dp(j - 1)
+            spread_ctx(j - 1)
 
         @pl.when(j >= 2)
         def _():
-            spread_ctx(j - 2)
+            spread_dp(j - 2)
 
     each(tiles, one_tile)
     if tiles >= 2:
-        spread_ctx(tiles - 2)
+        spread_dp(tiles - 2)
+    spread_ctx(tiles - 1)
     spread_dp(tiles - 1)
-    spread_ctx(tiles - 1)
 
     def finish(j):
         for a in range(2):
@@ -297,9 +297,9 @@
                 lambda i: out_copy(a, j, i + 1, lax.rem(me + nctx - i - 1, nctx)).wait_recv(),
             )
         each(ndp - 1, lambda i: rs_copy(j, i + 1).wait_send())
+        each(nctx - 1, lambda i: gc_copy(j, i + 1, me).wait_send())
         each(ndp - 1, lambda i: gd_copy(j, i + 1, dp).wait_send())
-        each(nctx - 1, lambda i: gc_copy(j, i + 1, me).wait_send())
-        each(nctx - 1, lambda i: gc_copy(j, i + 1, lax.rem(me + nctx - i - 1, nctx)).wait_recv())
+        each(ndp - 1, lambda i: gd_copy(j, i + 1, lax.rem(dp + ndp - i - 1, ndp)).wait_recv())
 
     each(tiles, finish)
 
@@ -321,7 +321,7 @@
     taps = lax.dynamic_slice_in_dim(masked, me * units, units, 1).T.astype(jnp.float32)
     wt = lax.dynamic_slice_in_dim(short_weights.reshape(9, channels), me * width, width, 1).T
     filled = reach * tile_units + UNIT
-    chunk = -(-filled // (8 * ndp)) * 8
+    chunk = -(-filled // (UNIT * ndp)) * UNIT
     hbm = pl.BlockSpec(memory_space=pltpu.HBM)
     vmem = pl.BlockSpec(memory_space=pltpu.VMEM)
     dma = pltpu.SemaphoreType.DMA
@@ -333,7 +333,7 @@
         out_shape=[
             jax.ShapeDtypeStruct((rows, channels), jnp.bfloat16),
             jax.ShapeDtypeStruct((rows, channels), jnp.bfloat16),
-            jax.ShapeDtypeStruct((nctx, tiles, ndp, chunk, PANEL), jnp.float32),
+            jax.ShapeDtypeStruct((tiles, ndp, nctx, chunk, PANEL), jnp.bfloat16),
         ],
         scratch_shapes=[
             pltpu.VMEM((2, nctx, PANEL, width), jnp.bfloat16),
@@ -347,7 +347,7 @@
             pltpu.VMEM((TILE, PANEL), jnp.float32),
             pltpu.VMEM((tiles, ndp, chunk, PANEL), jnp.float32),
             pltpu.VMEM((tiles, ndp, chunk, PANEL), jnp.float32),
-            pltpu.VMEM((tiles, chunk, PANEL), jnp.float32),
+            pltpu.VMEM((tiles, chunk, PANEL), jnp.bfloat16),
             dma((2, tiles)),
             dma((2, tiles, nctx)),
             dma((2, tiles, nctx)),
@@ -363,10 +363,10 @@
             dma((tiles, nctx)),
         ],
         compiler_params=pltpu.CompilerParams(
-            collective_id=0, has_side_effects=True, vmem_limit_bytes=63 * 2**20
+            collective_id=0, has_side_effects=True, vmem_limit_bytes=40 * 2**20
         ),
     )(features[0], cotangent[0], wt, taps)
-    every = every.reshape(nctx, tiles, ndp * chunk, PANEL)
+    every = every.astype(jnp.float32).transpose(2, 0, 1, 3, 4).reshape(nctx, tiles, ndp * chunk, PANEL)
     lag_rows = every[:, :, : reach * tile_units].reshape(nctx, tiles, reach, tile_units, PANEL)
     filter_sum = lag_rows.transpose(2, 4, 0, 1, 3).reshape(filter_len, groups)
     filter_grad = jnp.where(keep, filter_sum, jnp.zeros((), jnp.float32))

time: 78.5 us -> 75.3 us (0.959)
  Pallas kernels: 67.9 us -> 65.9 us
  local copies, waits for them, and re-layouts: 8.58 us -> 7.26 us
    pallas_call x1, Pallas kernels: 67.9 us -> 65.9 us  [shards(): pl.pallas_call(functools.partial(layer_kernel, reach, ndp, nctx), in_spec...]
    slice x1, local copies, waits for them, and re-layouts: 1.09 us -> 0.04 us  [shards(): every[:, :, :reach * tile_units]]
    transpose x2, local copies, waits for them, and re-layouts: 1.04 us -> 0.08 us  [shards(): short_grad = short_rows.transpose(2, 0, 1, 3).reshape(3, 3, channels)]
    reshape x1, local copies, waits for them, and re-layouts: 0.07 us -> 1 us  [shards(): short_weights.reshape(9, channels)]
where the time goes in v4:
time: 75.3 us; the launch traced here: 75.1 us
  Pallas kernels  65.9 us (88%)
  local copies, waits for them, and re-layouts  7.26 us (10%)
  other arithmetic  1.14 us (2%)
  between operations  0.8 us (1%)
    pallas_call x1, Pallas kernels, shards(): pl.pallas_call(functools.partial(layer_kernel, reach, ndp, nctx), in_spec...  65.9 us
    unnamed x15, local copies, waits for them, and re-layouts  5.11 us

profile of v4, /device:TPU:0, one launch (start us, length us, event | category | flops | bytes accessed | tf_op | source)
XLA Modules:
  0.0 75.1 jit_solution(17889114203140901034)
XLA Ops:
  0.6 0.0 copy-start
  0.6 0.0 copy-start.1
  0.7 0.8 %broadcast_multiply_fusion = s32[256]{0:T(256)S(1)} fusion(s32[256]{0:T(256)} %param.8), kind=kLoop, calls=%fused_computation.8 | loop fusion | flops 256 | bytes 2048 | tf_op jit(solution)/shard_map/mul | solution.py:312
  1.4 0.1 iota_compare_fusion
  1.6 0.0 copy-done
  1.6 0.1 constant_dynamic-slice_fusion
  1.7 0.1 copy.23
  1.8 1.0 %reshape.28 = f32[9,4096]{1,0:T(8,128)S(1)} reshape(f32[3,3,4096]{2,1,0:T(4,128)} %param.6) | data formatting | bytes 294912 | tf_op jit(solution)/shard_map/reshape | solution.py:322
  2.9 0.1 copy.22
  3.0 0.0 copy-done.1
  3.0 0.0 copy-start.2
  3.0 1.2 %copy-done.2 = bf16[1,128,4096]{2,1,0:T(8,128)(2,1)S(1)} copy-done((bf16[1,128,4096]{2,1,0:T(8,128)(2,1)S(1)}, bf16[1,128,4096]{2,1,0:T(8,128)(2,1)}, u32[]{:S(2)}) %copy-start.2) | copy-done | bytes 1048600
  4.2 65.9 %shard_map.84 = (bf16[128,4096]{1,0:T(8,128)(2,1)S(1)}, bf16[128,4096]{1,0:T(8,128)(2,1)S(1)}, bf16[4,4,8,16,128]{4,3,2,1,0:T(8,128)(2,1)S(1)}) custom-call(bf16[128,4096]{1,0:T(8,128)(2,1)S(1)} %bitcast.17, bf16[128,4096]{1,0:T(8,128)(2,1)S(1)} %bitcast.18, f32[512,9]{1,0:T(8,128)S(1)} %bitcast.19, f32[32,512]{1,0:T(8,128)S(1)} %convert_bitcast_fusion.1.taps), custom_call_target="tpu_custom_call" | custom-call | tf_op jit(solution)/shard_map/pallas_call | solution.py:329
  70.2 0.0 copy-start.3
  70.2 0.1 convert_bitcast_fusion
  70.3 0.1 copy.19
  70.4 0.7 copy-done.3
  71.2 0.1 copy.20
  71.3 0.0 copy-start.4
  71.3 0.1 broadcast_select_fusion
  71.4 1.0 %copy.21 = f32[512,256]{1,0:T(8,128)} copy(f32[512,256]{0,1:T(8,128)S(1)} %broadcast_select_fusion) | data formatting | bytes 1048576
  72.4 0.8 %reshape.33 = f32[3,3,4096]{2,1,0:T(4,128)} reshape(f32[9,8,4,128]{3,2,1,0:T(4,128)S(1)} %copy.20) | data formatting | bytes 294912 | tf_op jit(solution)/shard_map/reshape | solution.py:374
  73.2 0.0 copy-done.4
  73.2 1.0 %copy.26 = bf16[1,128,4096]{2,1,0:T(8,128)(2,1)} copy(bf16[1,128,4096]{2,1,0:T(8,128)(2,1)S(1)} %bitcast.21) | data formatting | bytes 2097152
  74.2 1.0 %copy.27 = bf16[1,128,4096]{2,1,0:T(8,128)(2,1)} copy(bf16[1,128,4096]{2,1,0:T(8,128)(2,1)S(1)} %bitcast.20) | data formatting | bytes 2097152
  (4 shorter events, 0.1 us)
Async XLA Ops:
  0.6 1.0 %copy-start = (bf16[512,256]{1,0:T(8,128)(2,1)S(1)}, bf16[512,256]{1,0:T(8,128)(2,1)}, u32[]{:S(2)}) copy-start(bf16[512,256]{1,0:T(8,128)(2,1)} %param.7) | copy-start | bytes 786436
  0.6 2.4 %copy-start.1 = (bf16[1,128,4096]{2,1,0:T(8,128)(2,1)S(1)}, bf16[1,128,4096]{2,1,0:T(8,128)(2,1)}, u32[]{:S(2)}) copy-start(bf16[1,128,4096]{2,1,0:T(8,128)(2,1)} %param.5) | copy-start | bytes 3145732
  3.0 1.2 %copy-start.2 = (bf16[1,128,4096]{2,1,0:T(8,128)(2,1)S(1)}, bf16[1,128,4096]{2,1,0:T(8,128)(2,1)}, u32[]{:S(2)}) copy-start(bf16[1,128,4096]{2,1,0:T(8,128)(2,1)} %param.9) | copy-start | bytes 3145732
  70.2 1.0 %copy-start.3 = (bf16[128,4096]{1,0:T(8,128)(2,1)}, bf16[128,4096]{1,0:T(8,128)(2,1)S(1)}, u32[]{:S(2)}) copy-start(bf16[128,4096]{1,0:T(8,128)(2,1)S(1)} %get-tuple-element.7) | copy-start | bytes 3145732
  71.3 1.9 %copy-start.4 = (bf16[128,4096]{1,0:T(8,128)(2,1)S(1)}, bf16[128,4096]{1,0:T(8,128)(2,1)}, u32[]{:S(2)}) copy-start(bf16[128,4096]{1,0:T(8,128)(2,1)} %copy-done.3) | copy-start | bytes 3145732

commit v5 on v4

--- a/solution.py
+++ b/solution.py
@@ -218,7 +218,8 @@
         for a in range(2):
             each(nctx - 1, lambda i: in_copy(a, j, i + 1, me).start())
 
-    each(tiles, send_in)
+    ahead = min(2, tiles)
+    each(ahead, send_in)
 
     def build(g):
         spreads[g] = toeplitz(taps[pl.ds(g, 1), :])
@@ -246,6 +247,10 @@
                 nctx - 1,
                 lambda i: in_copy(a, j, i + 1, lax.rem(me + nctx - i - 1, nctx)).wait_recv(),
             )
+
+        @pl.when(j + ahead < tiles)
+        def _():
+            send_in(j + ahead)
 
         def turn_in(n):
             ft[n] = arrived[0, n, :, lanes(j)].astype(jnp.float32).T

time: 75.3 us -> 75.3 us (level)
  no operation moved by 1% of the time
where the time goes in v5:
time: 75.3 us; the launch traced here: 75.1 us
  Pallas kernels  65.9 us (88%)
  local copies, waits for them, and re-layouts  7.26 us (10%)
  other arithmetic  1.14 us (2%)
  between operations  0.8 us (1%)
    pallas_call x1, Pallas kernels, shards(): pl.pallas_call(functools.partial(layer_kernel, reach, ndp, nctx), in_spec...  65.9 us
    unnamed x15, local copies, waits for them, and re-layouts  5.11 us

profile of v5, /device:TPU:0, one launch (start us, length us, event | category | flops | bytes accessed | tf_op | source)
XLA Modules:
  0.0 75.1 jit_solution(12328917736328694155)
XLA Ops:
  0.6 0.0 copy-start
  0.6 0.0 copy-start.1
  0.7 0.8 %broadcast_multiply_fusion = s32[256]{0:T(256)S(1)} fusion(s32[256]{0:T(256)} %param.8), kind=kLoop, calls=%fused_computation.8 | loop fusion | flops 256 | bytes 2048 | tf_op jit(solution)/shard_map/mul | solution.py:317
  1.4 0.1 iota_compare_fusion
  1.6 0.0 copy-done
  1.6 0.1 constant_dynamic-slice_fusion
  1.7 0.1 copy.23
  1.8 1.0 %reshape.28 = f32[9,4096]{1,0:T(8,128)S(1)} reshape(f32[3,3,4096]{2,1,0:T(4,128)} %param.6) | data formatting | bytes 294912 | tf_op jit(solution)/shard_map/reshape | solution.py:327
  2.9 0.1 copy.22
  3.0 0.0 copy-done.1
  3.0 0.0 copy-start.2
  3.0 1.2 %copy-done.2 = bf16[1,128,4096]{2,1,0:T(8,128)(2,1)S(1)} copy-done((bf16[1,128,4096]{2,1,0:T(8,128)(2,1)S(1)}, bf16[1,128,4096]{2,1,0:T(8,128)(2,1)}, u32[]{:S(2)}) %copy-start.2) | copy-done | bytes 1048600
  4.2 65.9 %shard_map.84 = (bf16[128,4096]{1,0:T(8,128)(2,1)S(1)}, bf16[128,4096]{1,0:T(8,128)(2,1)S(1)}, bf16[4,4,8,16,128]{4,3,2,1,0:T(8,128)(2,1)S(1)}) custom-call(bf16[128,4096]{1,0:T(8,128)(2,1)S(1)} %bitcast.17, bf16[128,4096]{1,0:T(8,128)(2,1)S(1)} %bitcast.18, f32[512,9]{1,0:T(8,128)S(1)} %bitcast.19, f32[32,512]{1,0:T(8,128)S(1)} %convert_bitcast_fusion.1.taps), custom_call_target="tpu_custom_call" | custom-call | tf_op jit(solution)/shard_map/pallas_call | solution.py:334
  70.2 0.0 copy-start.3
  70.2 0.1 convert_bitcast_fusion
  70.3 0.1 copy.19
  70.4 0.7 copy-done.3
  71.2 0.1 copy.20
  71.3 0.0 copy-start.4
  71.3 0.1 broadcast_select_fusion
  71.4 1.0 %copy.21 = f32[512,256]{1,0:T(8,128)} copy(f32[512,256]{0,1:T(8,128)S(1)} %broadcast_select_fusion) | data formatting | bytes 1048576
  72.4 0.8 %reshape.33 = f32[3,3,4096]{2,1,0:T(4,128)} reshape(f32[9,8,4,128]{3,2,1,0:T(4,128)S(1)} %copy.20) | data formatting | bytes 294912 | tf_op jit(solution)/shard_map/reshape | solution.py:379
  73.2 0.0 copy-done.4
  73.2 1.0 %copy.26 = bf16[1,128,4096]{2,1,0:T(8,128)(2,1)} copy(bf16[1,128,4096]{2,1,0:T(8,128)(2,1)S(1)} %bitcast.21) | data formatting | bytes 2097152
  74.1 1.0 %copy.27 = bf16[1,128,4096]{2,1,0:T(8,128)(2,1)} copy(bf16[1,128,4096]{2,1,0:T(8,128)(2,1)S(1)} %bitcast.20) | data formatting | bytes 2097152
  (4 shorter events, 0.1 us)
Async XLA Ops:
  0.6 1.0 %copy-start = (bf16[512,256]{1,0:T(8,128)(2,1)S(1)}, bf16[512,256]{1,0:T(8,128)(2,1)}, u32[]{:S(2)}) copy-start(bf16[512,256]{1,0:T(8,128)(2,1)} %param.7) | copy-start | bytes 786436
  0.6 2.4 %copy-start.1 = (bf16[1,128,4096]{2,1,0:T(8,128)(2,1)S(1)}, bf16[1,128,4096]{2,1,0:T(8,128)(2,1)}, u32[]{:S(2)}) copy-start(bf16[1,128,4096]{2,1,0:T(8,128)(2,1)} %param.5) | copy-start | bytes 3145732
  3.0 1.2 %copy-start.2 = (bf16[1,128,4096]{2,1,0:T(8,128)(2,1)S(1)}, bf16[1,128,4096]{2,1,0:T(8,128)(2,1)}, u32[]{:S(2)}) copy-start(bf16[1,128,4096]{2,1,0:T(8,128)(2,1)} %param.9) | copy-start | bytes 3145732
  70.2 1.0 %copy-start.3 = (bf16[128,4096]{1,0:T(8,128)(2,1)}, bf16[128,4096]{1,0:T(8,128)(2,1)S(1)}, u32[]{:S(2)}) copy-start(bf16[128,4096]{1,0:T(8,128)(2,1)S(1)} %get-tuple-element.7) | copy-start | bytes 3145732
  71.3 1.9 %copy-start.4 = (bf16[128,4096]{1,0:T(8,128)(2,1)S(1)}, bf16[128,4096]{1,0:T(8,128)(2,1)}, u32[]{:S(2)}) copy-start(bf16[128,4096]{1,0:T(8,128)(2,1)} %copy-done.3) | copy-start | bytes 3145732
